TPU v7x, 32 devices: a whole 2x2x4 slice. The times are simulated.
32 devices in a mesh: parts: 2 (over y), ctx: 4 (over z), head: 2 (over x), fsdp: 2 (over core).
Axes of the slice: x: 2, y: 2, z: 4, core: 2. Of those that a mesh axis runs over, the one named last changes fastest.
Arguments:
- mixer_input_channels: bfloat16 [4096, 4096], P(('parts', 'ctx'), ('head', 'fsdp')), parts along dimension 0, may hold values from -6 to 6
- gate_channels: bfloat16 [4096, 4096], P(('parts', 'ctx'), ('head', 'fsdp')), parts along dimension 0, may hold values from -6 to 6
- input_group_maps: bfloat16 [4096, 1024], P(('parts', 'ctx'), ('head', 'fsdp')), parts along dimension 0, may hold values from -6 to 6
- output_group_maps: bfloat16 [4096, 1024], P(('parts', 'ctx'), ('head', 'fsdp')), parts along dimension 0, may hold values from -6 to 6
- step_size_input: float32 [64, 4096], P(('head', 'fsdp'), ('parts', 'ctx')), parts along dimension 1, may hold values from -4 to 4
- resets: int32 [4096], P(('parts', 'ctx')), parts along dimension 0, may hold values 0 or 1
- head_decay_rate: float32 [64], P(('head', 'fsdp')), may hold values from 2e-07 to 0.035
- step_size_bias: float32 [64], P(('head', 'fsdp')), may hold values from -1 to 1
- skip: float32 [64], P(('head', 'fsdp')), may hold values from 0.5 to 1.5
- gated_norm_gain: float32 [4096], P(('head', 'fsdp')), may hold values from 0.5 to 1.5
- adapter_down_map: bfloat16 [4096, 64], P(('head', 'fsdp')), may hold values from -0.09375 to 0.09375
- adapter_up_map: bfloat16 [64, 4096], P(None, ('head', 'fsdp')), may hold values from -0.75 to 0.75
- frozen_mixed_gradient: bfloat16 [4096, 4096], P(('parts', 'ctx'), ('head', 'fsdp')), parts along dimension 0, may hold values from -6 to 6
- layer_output_gradient: bfloat16 [4096, 4096], P(('parts', 'ctx'), ('head', 'fsdp')), parts along dimension 0, may hold values from -6 to 6
Outputs:
- mixed: bfloat16 [4096, 4096], P(('parts', 'ctx'), ('head', 'fsdp')), parts along dimension 0
- adapter_output: bfloat16 [4096, 4096], P(('parts', 'ctx'), ('head', 'fsdp')), parts along dimension 0
- mixer_input_gradient: bfloat16 [4096, 4096], P(('parts', 'ctx'), ('head', 'fsdp')), parts along dimension 0
- gate_input_gradient: bfloat16 [4096, 4096], P(('parts', 'ctx'), ('head', 'fsdp')), parts along dimension 0
- input_maps_gradient: bfloat16 [4096, 1024], P(('parts', 'ctx'), ('head', 'fsdp')), parts along dimension 0
- output_maps_gradient: bfloat16 [4096, 1024], P(('parts', 'ctx'), ('head', 'fsdp')), parts along dimension 0
- step_size_gradient: float32 [64, 4096], P(('head', 'fsdp'), ('parts', 'ctx')), parts along dimension 1
- adapter_down_gradient: float32 [8192, 64], P(('parts', 'head', 'fsdp')), parts along dimension 0
- adapter_up_gradient: float32 [128, 4096], P('parts', ('head', 'fsdp')), parts along dimension 0
There are 2 independent parts, one for each index of `parts`. A program takes and returns all parts, laid end to end along the dimension named above; an argument that names none is the same for every part. Nothing has to cross between parts.
All inputs are finite; a program needn't handle non-finite values. No bound on the sum of `resets` on one device may be relied on, other than what follows from the above.
Results may differ from a plain program's by a relative error of at most 0.0057.
Values sent between devices are 32-bit elements; how exact they have to be, the bound alone decides.
A program may use at most 128 MiB of HBM per device.

v0:
```python
import jax
import jax.numpy as jnp
from jax import lax
from jax.experimental import pallas as pl
from jax.experimental.pallas import tpu as pltpu
from jax.sharding import PartitionSpec as P

STATE = 128
LANES = 128
eps = 1e-05
adapter_scale = 2.0
highest = lax.Precision.HIGHEST
f32 = jnp.float32
bf16 = jnp.bfloat16


def nn(a, b):
    return lax.dot_general(a, b, (((1,), (0,)), ((), ())), preferred_element_type=f32)


def nt(a, b):
    return lax.dot_general(a, b, (((1,), (1,)), ((), ())), preferred_element_type=f32)


def tn(a, b):
    return lax.dot_general(a, b, (((0,), (0,)), ((), ())), preferred_element_type=f32)


def split(a):
    hi = a.astype(bf16)
    return hi, (a - hi.astype(f32)).astype(bf16)


def iota(shape, dim):
    return lax.broadcasted_iota(jnp.int32, shape, dim)


def expand(cols, group, per_group, width):
    pick = (iota((LANES, width), 0) == group * per_group + iota((LANES, width), 1) // (width // per_group))
    pick = jnp.where(pick, 1.0, 0.0).astype(bf16)
    hi, lo = split(cols)
    return nn(hi, pick) + nn(lo, pick)


def headsum(values, group, per_group):
    width = values.shape[1]
    pick = (iota((width, LANES), 1) == group * per_group + iota((width, LANES), 0) // (width // per_group))
    pick = jnp.where(pick, 1.0, 0.0).astype(bf16)
    hi, lo = split(values)
    return nn(hi, pick) + nn(lo, pick)


def score_mask(rid_col, rid_row):
    n = rid_col.shape[0]
    return (rid_col == rid_row) & (iota((n, n), 0) >= iota((n, n), 1))


def scan_kernel(x_ref, b_ref, dtin_ref, bias_ref, rate_ref, resets_ref,
                e_ref, einv_ref, dt_ref, rc_ref, rr_ref, em_ref, state_ref):
    rows = x_ref.shape[0]
    heads = dtin_ref.shape[0]
    groups = b_ref.shape[1] // STATE
    per_group = heads // groups
    width = x_ref.shape[1] // groups
    v = dtin_ref[...] + bias_ref[...]
    dt = jnp.maximum(v, 0.0) + jnp.log1p(jnp.exp(-jnp.abs(v)))
    log_step = -rate_ref[...] * dt
    marks = jnp.broadcast_to(resets_ref[...].astype(f32), (8, rows))
    stack = jnp.concatenate([log_step, marks, jnp.zeros((LANES - heads - 8, rows), f32)], axis=0)
    dt_cols = jnp.concatenate([dt, jnp.zeros((LANES - heads, rows), f32)], axis=0).T
    tri = jnp.where(iota((rows, rows), 0) >= iota((rows, rows), 1), 1.0, 0.0)
    cum = lax.dot_general(tri, stack.T, (((1,), (0,)), ((), ())), precision=highest, preferred_element_type=f32)
    cum_rows = cum.T
    rid_col = cum[:, heads : heads + 1]
    rid_row = cum_rows[heads : heads + 1, :]
    rid_last = cum[rows - 1 : rows, heads : heads + 1]
    cum_heads = jnp.where(iota((rows, LANES), 1) < heads, cum, 0.0)
    mid = 0.5 * cum_heads[rows - 1 : rows, :]
    e_ref[...] = jnp.exp(cum_heads - mid)
    einv = jnp.exp(mid - cum_heads)
    einv_ref[...] = einv
    dt_ref[...] = dt_cols
    f_cols = dt_cols * einv
    rc_ref[...] = jnp.broadcast_to(rid_col, rc_ref.shape)
    rr_ref[...] = jnp.broadcast_to(rid_row, rr_ref.shape)
    ends = rid_col == rid_last
    unbroken = jnp.where(rid_last == 0, 1.0, 0.0)
    em_cols = jnp.broadcast_to(jnp.exp(mid), (8, LANES))
    for g in range(groups):
        cols = slice(g * width, (g + 1) * width)
        em = expand(em_cols, g, per_group, width)
        xd = (x_ref[:, cols].astype(f32) * expand(f_cols, g, per_group, width)).astype(bf16)
        b_end = jnp.where(ends, b_ref[:, g * STATE : (g + 1) * STATE], 0.0).astype(bf16)
        em_ref[:, cols] = em
        state_ref[:STATE, cols] = em[:1] * tn(b_end, xd)
        state_ref[STATE:, cols] = em * em * unbroken


def forward_kernel(ctx, heads, place_ref, x_ref, z_ref, b_ref, c_ref, gx_ref, e_ref, einv_ref, dt_ref, rc_ref,
                   rr_ref, em_ref, skip_ref, gain_ref, down_ref, gu_ref, gathered_ref,
                   mixed_ref, dz_ref, gy_ref, gd_ref, sin_ref, ginj_ref, pn_ref, k_ref, ddown_ref, u_ref):
    rows = x_ref.shape[0]
    groups = b_ref.shape[1] // STATE
    width = x_ref.shape[1] // groups
    per_group = heads // groups
    place = place_ref[0]

    sin_ref[...] = jnp.zeros_like(sin_ref)

    def fold(j, _):
        sin_ref[...] = gathered_ref[j, STATE : STATE + 1, :] * sin_ref[...] + gathered_ref[j, :STATE, :]
        return 0

    lax.fori_loop(0, place, fold, 0)
    mask = score_mask(rc_ref[:, :1], rr_ref[:1, :])
    fresh = rc_ref[:, :1] == 0
    f_cols = dt_ref[...] * einv_ref[...]
    gu = gu_ref[...]
    u = jnp.zeros(u_ref.shape, f32)
    pn = jnp.zeros(pn_ref.shape, f32)
    kk = jnp.zeros((8, LANES), f32)
    for g in range(groups):
        cols = slice(g * width, (g + 1) * width)
        narrow = slice(g * STATE, (g + 1) * STATE)
        x = x_ref[:, cols].astype(f32)
        ex = expand(e_ref[...], g, per_group, width)
        xd = (x * expand(f_cols, g, per_group, width)).astype(bf16)
        c = c_ref[:, narrow]
        a = jnp.where(mask, nt(c, b_ref[:, narrow]), 0.0).astype(bf16)
        c0 = jnp.where(fresh, c, 0.0).astype(bf16)
        em = em_ref[:1, cols]
        s = (em * sin_ref[:, cols]).astype(bf16)
        inner = nn(a, xd) + nn(c0, s)
        y = ex * inner + skip_ref[:, cols] * x
        z = z_ref[:, cols].astype(f32)
        sig = 1.0 / (1.0 + jnp.exp(-z))
        act = z * sig
        gated = y * act
        inv = lax.rsqrt(jnp.mean(gated * gated, axis=-1, keepdims=True) + eps)
        normed = gated * inv
        gain = gain_ref[:, cols]
        mixed = (normed * gain).astype(bf16)
        mixed_ref[:, cols] = mixed
        down = down_ref[cols, :]
        u = u + nn(mixed, down)
        ddown_ref[cols, :] = tn(mixed, gu)
        gn = (gx_ref[:, cols].astype(f32) + nt(gu, down)) * gain
        gg = inv * (gn - normed * jnp.mean(gn * normed, axis=-1, keepdims=True))
        gy = gg * act
        dz_ref[:, cols] = (gg * y * sig * (1.0 + z * (1.0 - sig))).astype(bf16)
        gy_ref[:, cols] = gy
        gd = (gy * ex).astype(bf16)
        gd_ref[:, cols] = gd
        inj = tn(c0, gd)
        ginj_ref[:STATE, cols] = em * inj
        pn = pn + headsum(gd.astype(f32) * inner, g, per_group)
        kk = kk + headsum(jnp.broadcast_to(jnp.sum(s.astype(f32) * inj, axis=0, keepdims=True), (8, width)), g, per_group)
    ginj_ref[STATE:, :] = gathered_ref[place, STATE:, :]
    u_ref[...] = u
    pn_ref[...] = pn
    k_ref[...] = kk


def backward_kernel(ctx, heads, place_ref, x_ref, b_ref, c_ref, e_ref, einv_ref, dt_ref, rc_ref, rr_ref, em_ref,
                    skip_ref, rate_ref, gy_ref, gd_ref, sin_ref, pn_ref, k_ref, gathered_ref,
                    dx_ref, db_ref, dc_ref, dstep_ref, gin_ref):
    rows = x_ref.shape[0]
    groups = b_ref.shape[1] // STATE
    width = x_ref.shape[1] // groups
    per_group = heads // groups
    place = place_ref[0]

    gin_ref[...] = jnp.zeros_like(gin_ref)

    def fold(i, _):
        j = ctx - 1 - i
        gin_ref[...] = gathered_ref[j, STATE : STATE + 1, :] * gin_ref[...] + gathered_ref[j, :STATE, :]
        return 0

    lax.fori_loop(0, ctx - 1 - place, fold, 0)
    decay_row = gathered_ref[place, STATE : STATE + 1, :]
    mask = score_mask(rc_ref[:, :1], rr_ref[:1, :])
    fresh = rc_ref[:, :1] == 0
    ends = rc_ref[:, :1] == rc_ref[rows - 1 : rows, :1]
    f_cols = dt_ref[...] * einv_ref[...]
    net = -pn_ref[...]
    step = jnp.zeros(pn_ref.shape, f32)
    kk = k_ref[...]
    for g in range(groups):
        cols = slice(g * width, (g + 1) * width)
        narrow = slice(g * STATE, (g + 1) * STATE)
        x = x_ref[:, cols].astype(f32)
        fx = expand(f_cols, g, per_group, width)
        xd = (x * fx).astype(bf16)
        gd = gd_ref[:, cols]
        b = b_ref[:, narrow]
        c = c_ref[:, narrow]
        a = jnp.where(mask, nt(c, b), 0.0).astype(bf16)
        b_end = jnp.where(ends, b, 0.0).astype(bf16)
        em = em_ref[:1, cols]
        sin = sin_ref[:, cols]
        gin = gin_ref[:, cols]
        s = (em * sin).astype(bf16)
        ge = (em * gin).astype(bf16)
        v = tn(a, gd) + nn(b_end, ge)
        dx_ref[:, cols] = (fx * v + skip_ref[:, cols] * gy_ref[:, cols]).astype(bf16)
        pair = jnp.where(mask, nt(gd, xd), 0.0).astype(bf16)
        dc_ref[:, narrow] = (nn(pair, b) + jnp.where(fresh, nt(gd, s), 0.0)).astype(bf16)
        db_ref[:, narrow] = (tn(pair, c) + jnp.where(ends, nt(xd, ge), 0.0)).astype(bf16)
        net = net + headsum(xd.astype(f32) * v, g, per_group)
        step = step + headsum(x * v, g, per_group)
        through = decay_row[:, cols] * jnp.sum(sin * gin, axis=0, keepdims=True)
        kk = kk + headsum(jnp.broadcast_to(through, (8, width)), g, per_group)
    before = jnp.where(iota((rows, rows), 0) > iota((rows, rows), 1), 1.0, 0.0)
    glog = lax.dot_general(before, net, (((1,), (0,)), ((), ())), precision=highest, preferred_element_type=f32) + kk[:1]
    gdt = einv_ref[...] * step - rate_ref[...] * glog
    out = gdt * (1.0 - jnp.exp(-dt_ref[...]))
    dstep_ref[...] = out.T[: dstep_ref.shape[0], :]


def vm():
    return pl.BlockSpec(memory_space=pltpu.VMEM)


def call(kernel, name, outs, args, scalars=0):
    specs = [pl.BlockSpec(memory_space=pltpu.SMEM)] * scalars + [vm()] * (len(args) - scalars)
    return pl.pallas_call(
        kernel,
        name=name,
        out_shape=[jax.ShapeDtypeStruct(s, d) for s, d in outs],
        in_specs=specs,
        out_specs=[vm()] * len(outs),
        compiler_params=pltpu.CompilerParams(vmem_limit_bytes=56 << 20),
    )(*args)


def per_device(x, z, b, c, dtin, resets, rate, bias, skip, gain, down, up, gx, gout):
    rows, channels = x.shape
    heads = dtin.shape[0]
    rank = down.shape[1]
    ctx = lax.axis_size("ctx")
    place = lax.axis_index("ctx").astype(jnp.int32).reshape(1)
    head_dim = channels // heads
    wide = STATE + 8
    gu_part = nt(gout, up)
    gu = (adapter_scale * lax.psum(gu_part, ("head", "fsdp"))).astype(bf16)
    skip_row = jnp.repeat(skip, head_dim)[None, :]
    gain_row = gain[None, :]
    rate_row = jnp.pad(rate, (0, LANES - heads))[None, :]
    e, einv, dt, rc, rr, em, state = call(
        scan_kernel, "scan",
        [((rows, LANES), f32)] * 4 + [((8, rows), f32), ((8, channels), f32), ((wide, channels), f32)],
        (x, b, dtin, bias[:, None], rate[:, None], resets[None, :]),
    )
    gathered = lax.all_gather(state, "ctx")
    mixed, dz, gy, gd, sin, ginj, pn, kk, ddown, u_part = call(
        lambda *r: forward_kernel(ctx, heads, *r), "forward",
        [((rows, channels), bf16), ((rows, channels), bf16), ((rows, channels), f32), ((rows, channels), bf16),
         ((STATE, channels), f32), ((wide, channels), f32), ((rows, LANES), f32), ((8, LANES), f32),
         ((channels, rank), f32), ((rows, rank), f32)],
        (place, x, z, b, c, gx, e, einv, dt, rc, rr, em, skip_row, gain_row, down, gu, gathered), 1,
    )
    back = lax.all_gather(ginj, "ctx")
    u = (adapter_scale * lax.psum(u_part, ("head", "fsdp"))).astype(bf16)
    adapter_output = nn(u, up).astype(bf16)
    dup = tn(u, gout)
    ddown, dup = lax.psum((ddown, dup), "ctx")
    dx, db, dc, dstep, _ = call(
        lambda *r: backward_kernel(ctx, heads, *r), "backward",
        [((rows, channels), bf16), (b.shape, bf16), (c.shape, bf16), ((heads, rows), f32), ((STATE, channels), f32)],
        (place, x, b, c, e, einv, dt, rc, rr, em, skip_row, rate_row, gy, gd, sin, pn, kk, back), 1,
    )
    return mixed, adapter_output, dx, dz, db, dc, dstep, ddown, dup


def solution(mesh):
    wide = P(("parts", "ctx"), ("head", "fsdp"))
    steps = P(("head", "fsdp"), ("parts", "ctx"))
    over_heads = P(("head", "fsdp"))
    in_specs = (
        wide, wide, wide, wide, steps, P(("parts", "ctx")), over_heads, over_heads, over_heads, over_heads,
        P(("head", "fsdp"), None), P(None, ("head", "fsdp")), wide, wide,
    )
    out_specs = (
        wide, wide, wide, wide, wide, wide, steps, P(("parts", "head", "fsdp"), None), P("parts", ("head", "fsdp")),
    )
    return jax.shard_map(per_device, mesh=mesh, in_specs=in_specs, out_specs=out_specs, check_vma=False)
```

profile of v0, /device:TPU:0, one launch (start us, length us, event | category | flops | bytes accessed | tf_op | source)
XLA Modules:
  0.0 228.7 jit_solution(2075408570854488292)
XLA Ops:
  8.0 0.0 copy-start
  8.0 0.0 copy-start.5
  8.0 0.0 copy-start.4
  8.0 0.0 all-reduce.6.cloned.1.call-start
  8.1 1.2 copy-done
  9.2 2.0 fusion.3
  11.3 0.0 all-reduce.6.cloned.1.call-update
  11.3 0.0 all-gather.5.cloned.1.call-start
  11.3 1.3 copy.23.bias_ref
  12.7 1.3 copy.24.rate_ref
  14.0 5.6 %scan.1 = (f32[512,128]{1,0:T(8,128)}, f32[512,128]{1,0:T(8,128)}, f32[512,128]{1,0:T(8,128)}, f32[512,128]{1,0:T(8,128)}, f32[8,512]{1,0:T(8,128)}, /*index=5*/f32[8,1024]{1,0:T(8,128)}, f32[136,1024]{1,0:T(8,128)}) custom-call(bf16[512,1024]{1,0:T(8,128)(2,1)} %r_1_.3, bf16[512,256]{1,0:T(8,128)(2,1)} %r_2_.3, f32[16,512]{1,0:T(8,128)} %dtin_ref.1, ...), custom_call_target="tpu_custom_call" | custom-call | tf_op jit(solution)/shard_map/scan/pallas_call | solution.py:227
  19.6 0.0 all-gather.5.cloned.1.call-update
  19.6 0.0 all-reduce.8.cloned.1.call-start
  19.7 0.0 copy-done.5
  19.7 0.1 broadcast_in_dim.21
  19.8 0.7 broadcast_in_dim_reshape.3.r_12_.r_10_
  20.4 0.0 copy-done.4
  20.4 0.8 copy.26.r_14_
  21.3 25.3 %all-reduce.6.cloned.1.call-done = f32[512,64]{1,0:T(8,128)} async-done(((f32[512,64]{1,0:T(8,128)}), f32[512,64]{1,0:T(8,128)}) %all-reduce.6.cloned.1.call-update) | async-done | bytes 131088 | tf_op jit(solution)/shard_map/psum | solution.py:246
  46.6 1.6 multiply_convert_fusion.1.r_15_
  48.2 21.9 %all-gather.5.cloned.1.call-done = f32[544,1024]{1,0:T(8,128)} async-done(((f32[136,1024]{1,0:T(8,128)}), f32[544,1024]{1,0:T(8,128)}) %all-gather.5.cloned.1.call-update) | async-done | bytes 2228240 | tf_op jit(solution)/shard_map/all_gather | solution.py:255
  70.2 12.0 %forward.1 = (bf16[512,1024]{1,0:T(8,128)(2,1)}, bf16[512,1024]{1,0:T(8,128)(2,1)}, f32[512,1024]{1,0:T(8,128)}, bf16[512,1024]{1,0:T(8,128)(2,1)}, f32[128,1024...) custom-call(s32[1]{0:T(128)} %bitcast.r_0_, ...), custom_call_target="tpu_custom_call" | custom-call | tf_op jit(solution)/shard_map/forward/pallas_call | solution.py:227
  82.1 0.0 copy-start.6
  82.2 0.0 copy-start.2
  82.2 0.0 all-reduce.8.cloned.1.call-update
  82.2 0.0 all-reduce.10.cloned.1.call-start
  82.2 31.1 %all-reduce.8.cloned.1.call-done = f32[512,64]{1,0:T(8,128)} async-done(((f32[512,64]{1,0:T(8,128)}), f32[512,64]{1,0:T(8,128)}) %all-reduce.8.cloned.1.call-update) | async-done | bytes 131088 | tf_op jit(solution)/shard_map/psum | solution.py:264
  113.3 0.0 copy-start.1
  113.3 2.0 fusion
  115.4 0.0 all-reduce.10.cloned.1.call-update
  115.4 0.0 all-gather.7.cloned.1.call-start
  115.4 0.5 all-gather.7.cloned.1.call-update
  116.0 0.0 copy-done.6
  116.0 0.6 pad_bitcast_fusion.r_11_
  116.5 0.0 copy-done.2
  116.5 0.0 copy-done.1
  116.5 1.4 convolution_convert_fusion
  117.9 41.5 %all-reduce.10.cloned.1.call-done = (f32[1024,64]{1,0:T(8,128)}, f32[64,1024]{1,0:T(8,128)}) async-done(((f32[1024,64]{1,0:T(8,128)}, f32[64,1024]{1,0:T(8,128)}), (f32[1024,64]{1,0:T(8,128)}, f32[64,1024]{1,0:T(8,128)})) %all-reduce.10.cloned.1.call-update) | async-done | bytes 524304 | tf_op jit(solution)/shard_map/psum | solution.py:267
  159.4 1.9 copy.27
  161.3 47.1 %all-gather.7.cloned.1.call-done = f32[544,1024]{1,0:T(8,128)} async-done(((f32[136,1024]{1,0:T(8,128)}), f32[544,1024]{1,0:T(8,128)}) %all-gather.7.cloned.1.call-update) | async-done | bytes 2228240 | tf_op jit(solution)/shard_map/all_gather | solution.py:263
  208.4 0.0 copy-start.3
  208.4 12.0 %backward.1 = (bf16[512,1024]{1,0:T(8,128)(2,1)}, bf16[512,256]{1,0:T(8,128)(2,1)}, bf16[512,256]{1,0:T(8,128)(2,1)}, f32[16,512]{1,0:T(8,128)}, f32[128,1024]{1,0:T(8,128)}) custom-call(s32[1]{0:T(128)} %bitcast.r_0_, bf16[512,1024]{1,0:T(8,128)(2,1)} %r_1_.3, bf16[512,256]{1,0:T(8,128)(2,1)} %r_2_.3, bf16[512,256]{1,0:T(8,128)(2,1)} %r_3_.3, ...), custom_call_target="tpu_custom_call" | custom-call | tf_op jit(solution)/shard_map/backward/pallas_call | solution.py:227
  220.4 0.0 copy-done.3
  220.4 0.7 copy.33
Async XLA Ops:
  8.0 1.2 copy-start
  8.0 11.7 %copy-start.5 = (f32[16]{0:T(128)S(1)}, f32[16]{0:T(128)}, u32[]{:S(2)}) copy-start(f32[16]{0:T(128)} %param.22) | copy-start | bytes 196
  8.0 12.4 %copy-start.4 = (bf16[1024,64]{0,1:T(8,128)(2,1)S(1)}, bf16[1024,64]{0,1:T(8,128)(2,1)}, u32[]{:S(2)}) copy-start(bf16[1024,64]{0,1:T(8,128)(2,1)} %param.24) | copy-start | bytes 393220
  8.0 38.6 %all-reduce.6.cloned.1.call-start = ((), (), s32[]{:S(2)}) async-start(), calls=%async_computation | async-start | bytes 524288 | tf_op jit(solution)/shard_map/psum | solution.py:246
  11.3 58.9 %all-gather.5.cloned.1.call-start = ((), (), s32[]{:S(2)}) async-start(), calls=%async_computation.2 | async-start | bytes 2785280 | tf_op jit(solution)/shard_map/all_gather | solution.py:255
  19.6 93.7 %all-reduce.8.cloned.1.call-start = ((), (), s32[]{:S(2)}) async-start(), calls=%async_computation.1 | async-start | bytes 524288 | tf_op jit(solution)/shard_map/psum | solution.py:264
  82.1 33.8 %copy-start.6 = (f32[16]{0:T(128)S(1)}, f32[16]{0:T(128)}, u32[]{:S(2)}) copy-start(f32[16]{0:T(128)} %param.20) | copy-start | bytes 196
  82.2 34.4 %copy-start.2 = (bf16[64,1024]{1,0:T(8,128)(2,1)S(1)}, bf16[64,1024]{1,0:T(8,128)(2,1)}, u32[]{:S(2)}) copy-start(bf16[64,1024]{1,0:T(8,128)(2,1)} %param.25) | copy-start | bytes 393220
  82.2 77.2 %all-reduce.10.cloned.1.call-start = ((), (), s32[]{:S(2)}) async-start(), calls=%async_computation.4 | async-start | bytes 1572864 | tf_op jit(solution)/shard_map/psum | solution.py:267
  113.3 3.2 %copy-start.1 = (f32[512,64]{1,0:T(8,128)S(1)}, f32[512,64]{1,0:T(8,128)}, u32[]{:S(2)}) copy-start(f32[512,64]{1,0:T(8,128)} %all-reduce.8.cloned.1.call-done) | copy-start | bytes 393220
  115.4 93.0 %all-gather.7.cloned.1.call-start = ((), (), s32[]{:S(2)}) async-start(), calls=%async_computation.3 | async-start | bytes 2785280 | tf_op jit(solution)/shard_map/all_gather | solution.py:263
  208.4 12.0 %copy-start.3 = (f32[64,1024]{1,0:T(8,128)S(1)}, f32[64,1024]{1,0:T(8,128)}, u32[]{:S(2)}) copy-start(f32[64,1024]{1,0:T(8,128)} %get-tuple-element.70) | copy-start | bytes 786436
Sparse Core Ops, SparseCore 0:
  11.8 34.7 all-reduce.5
  82.3 30.9 all-reduce.7
Sparse Core Ops, SparseCore 1:
  19.7 50.4 all-gather.4
  115.5 43.9 all-reduce.9
  161.4 46.9 all-gather.6
where the time goes:
time: 229 us
  waiting for transfers between devices  167 us (73%)
  Pallas kernels  29.6 us (13%)
  between operations  15.8 us (7%)
  local copies, waits for them, and re-layouts  8.63 us (4%)
  matrix products  5.46 us (2%)
    all_gather x1, waiting for transfers between devices, per_device(): back = lax.all_gather(ginj, 'ctx')  47.1 us
    psum x1, waiting for transfers between devices, per_device(): ddown, dup = lax.psum((ddown, dup), 'ctx')  41.5 us
    psum x1, waiting for transfers between devices, per_device(): u = (adapter_scale * lax.psum(u_part, ('head', 'fsdp'))).astype(bf16)  31.1 us
    pallas_call x3, Pallas kernels, call(): pl.pallas_call(kernel, name=name, out_shape=[jax.ShapeDtypeStruct(s, d) f...  29.6 us
    psum x1, waiting for transfers between devices, per_device(): gu = (adapter_scale * lax.psum(gu_part, ('head', 'fsdp'))).astype(bf16)  25.3 us
    all_gather x1, waiting for transfers between devices, per_device(): gathered = lax.all_gather(state, 'ctx')  21.9 us
    unnamed x17, local copies, waits for them, and re-layouts  4.66 us
  transfers between devices with their start and end apart: 5, of which 5 were waited for; matrix products, arithmetic and copies ran while one was open for 4% of the time, Pallas kernels for 2%

commit v1 on v0

--- a/solution.py
+++ b/solution.py
@@ -56,7 +56,7 @@
 
 
 def scan_kernel(x_ref, b_ref, dtin_ref, bias_ref, rate_ref, resets_ref,
-                e_ref, einv_ref, dt_ref, rc_ref, rr_ref, em_ref, state_ref):
+                e_ref, einv_ref, dt_ref, rc_ref, rr_ref, em_ref, decay_ref, state_ref):
     rows = x_ref.shape[0]
     heads = dtin_ref.shape[0]
     groups = b_ref.shape[1] // STATE
@@ -92,26 +92,17 @@
         xd = (x_ref[:, cols].astype(f32) * expand(f_cols, g, per_group, width)).astype(bf16)
         b_end = jnp.where(ends, b_ref[:, g * STATE : (g + 1) * STATE], 0.0).astype(bf16)
         em_ref[:, cols] = em
-        state_ref[:STATE, cols] = em[:1] * tn(b_end, xd)
-        state_ref[STATE:, cols] = em * em * unbroken
-
-
-def forward_kernel(ctx, heads, place_ref, x_ref, z_ref, b_ref, c_ref, gx_ref, e_ref, einv_ref, dt_ref, rc_ref,
-                   rr_ref, em_ref, skip_ref, gain_ref, down_ref, gu_ref, gathered_ref,
-                   mixed_ref, dz_ref, gy_ref, gd_ref, sin_ref, ginj_ref, pn_ref, k_ref, ddown_ref, u_ref):
+        state_ref[:, cols] = em[:1] * tn(b_end, xd)
+        decay_ref[:, cols] = em * em * unbroken
+
+
+def forward_kernel(heads, x_ref, z_ref, b_ref, c_ref, gx_ref, e_ref, einv_ref, dt_ref, rc_ref,
+                   rr_ref, em_ref, skip_ref, gain_ref, down_ref, gu_ref, sin_ref,
+                   mixed_ref, dz_ref, gy_ref, gd_ref, ginj_ref, pn_ref, k_ref, ddown_ref, u_ref):
     rows = x_ref.shape[0]
     groups = b_ref.shape[1] // STATE
     width = x_ref.shape[1] // groups
     per_group = heads // groups
-    place = place_ref[0]
-
-    sin_ref[...] = jnp.zeros_like(sin_ref)
-
-    def fold(j, _):
-        sin_ref[...] = gathered_ref[j, STATE : STATE + 1, :] * sin_ref[...] + gathered_ref[j, :STATE, :]
-        return 0
-
-    lax.fori_loop(0, place, fold, 0)
     mask = score_mask(rc_ref[:, :1], rr_ref[:1, :])
     fresh = rc_ref[:, :1] == 0
     f_cols = dt_ref[...] * einv_ref[...]
@@ -141,10 +132,10 @@
         gain = gain_ref[:, cols]
         mixed = (normed * gain).astype(bf16)
         mixed_ref[:, cols] = mixed
-        down = down_ref[cols, :]
-        u = u + nn(mixed, down)
-        ddown_ref[cols, :] = tn(mixed, gu)
-        gn = (gx_ref[:, cols].astype(f32) + nt(gu, down)) * gain
+        down = down_ref[:, cols]
+        u = u + nt(down, mixed)
+        ddown_ref[:, cols] = nn(gu, mixed)
+        gn = (gx_ref[:, cols].astype(f32) + tn(gu, down)) * gain
         gg = inv * (gn - normed * jnp.mean(gn * normed, axis=-1, keepdims=True))
         gy = gg * act
         dz_ref[:, cols] = (gg * y * sig * (1.0 + z * (1.0 - sig))).astype(bf16)
@@ -152,33 +143,21 @@
         gd = (gy * ex).astype(bf16)
         gd_ref[:, cols] = gd
         inj = tn(c0, gd)
-        ginj_ref[:STATE, cols] = em * inj
+        ginj_ref[:, cols] = em * inj
         pn = pn + headsum(gd.astype(f32) * inner, g, per_group)
         kk = kk + headsum(jnp.broadcast_to(jnp.sum(s.astype(f32) * inj, axis=0, keepdims=True), (8, width)), g, per_group)
-    ginj_ref[STATE:, :] = gathered_ref[place, STATE:, :]
     u_ref[...] = u
     pn_ref[...] = pn
     k_ref[...] = kk
 
 
-def backward_kernel(ctx, heads, place_ref, x_ref, b_ref, c_ref, e_ref, einv_ref, dt_ref, rc_ref, rr_ref, em_ref,
-                    skip_ref, rate_ref, gy_ref, gd_ref, sin_ref, pn_ref, k_ref, gathered_ref,
-                    dx_ref, db_ref, dc_ref, dstep_ref, gin_ref):
+def backward_kernel(heads, x_ref, b_ref, c_ref, e_ref, einv_ref, dt_ref, rc_ref, rr_ref, em_ref,
+                    skip_ref, rate_ref, gy_ref, gd_ref, sin_ref, pn_ref, k_ref, gin_ref, decay_ref,
+                    dx_ref, db_ref, dc_ref, dstep_ref):
     rows = x_ref.shape[0]
     groups = b_ref.shape[1] // STATE
     width = x_ref.shape[1] // groups
     per_group = heads // groups
-    place = place_ref[0]
-
-    gin_ref[...] = jnp.zeros_like(gin_ref)
-
-    def fold(i, _):
-        j = ctx - 1 - i
-        gin_ref[...] = gathered_ref[j, STATE : STATE + 1, :] * gin_ref[...] + gathered_ref[j, :STATE, :]
-        return 0
-
-    lax.fori_loop(0, ctx - 1 - place, fold, 0)
-    decay_row = gathered_ref[place, STATE : STATE + 1, :]
     mask = score_mask(rc_ref[:, :1], rr_ref[:1, :])
     fresh = rc_ref[:, :1] == 0
     ends = rc_ref[:, :1] == rc_ref[rows - 1 : rows, :1]
@@ -209,7 +188,7 @@
         db_ref[:, narrow] = (tn(pair, c) + jnp.where(ends, nt(xd, ge), 0.0)).astype(bf16)
         net = net + headsum(xd.astype(f32) * v, g, per_group)
         step = step + headsum(x * v, g, per_group)
-        through = decay_row[:, cols] * jnp.sum(sin * gin, axis=0, keepdims=True)
+        through = decay_ref[:1, cols] * jnp.sum(sin * gin, axis=0, keepdims=True)
         kk = kk + headsum(jnp.broadcast_to(through, (8, width)), g, per_group)
     before = jnp.where(iota((rows, rows), 0) > iota((rows, rows), 1), 1.0, 0.0)
     glog = lax.dot_general(before, net, (((1,), (0,)), ((), ())), precision=highest, preferred_element_type=f32) + kk[:1]
@@ -218,19 +197,229 @@
     dstep_ref[...] = out.T[: dstep_ref.shape[0], :]
 
 
-def vm():
-    return pl.BlockSpec(memory_space=pltpu.VMEM)
-
-
-def call(kernel, name, outs, args, scalars=0):
-    specs = [pl.BlockSpec(memory_space=pltpu.SMEM)] * scalars + [vm()] * (len(args) - scalars)
+CHUNK = 16
+
+
+def remote(src, dst, send, recv, target):
+    return pltpu.make_async_remote_copy(
+        src_ref=src, dst_ref=dst, send_sem=send, recv_sem=recv, device_id=target,
+        device_id_type=pl.DeviceIdType.MESH,
+    )
+
+
+def group_peers():
+    inner = lax.axis_size("fsdp")
+    count = lax.axis_size("head") * inner
+    me = lax.axis_index("head") * inner + lax.axis_index("fsdp")
+    ids = [lax.rem(me + d, count) for d in range(1, count)]
+    return [{"head": lax.div(i, inner), "fsdp": lax.rem(i, inner)} for i in ids]
+
+
+def greet():
+    ctx = lax.axis_size("ctx")
+    place = lax.axis_index("ctx")
+    barrier = pltpu.get_barrier_semaphore()
+    peers = group_peers()
+    for peer in peers:
+        pl.semaphore_signal(barrier, inc=1, device_id=peer, device_id_type=pl.DeviceIdType.MESH)
+
+    @pl.when(place > 0)
+    def _():
+        pl.semaphore_signal(barrier, inc=1, device_id={"ctx": place - 1}, device_id_type=pl.DeviceIdType.MESH)
+
+    @pl.when(place < ctx - 1)
+    def _():
+        pl.semaphore_signal(barrier, inc=1, device_id={"ctx": place + 1}, device_id_type=pl.DeviceIdType.MESH)
+
+    ends = (place == 0) | (place == ctx - 1)
+
+    @pl.when(ends)
+    def _():
+        pl.semaphore_wait(barrier, len(peers) + 1)
+
+    @pl.when(jnp.logical_not(ends))
+    def _():
+        pl.semaphore_wait(barrier, len(peers) + 2)
+
+
+def exchange(part_ref, box, send, recv):
+    return [remote(part_ref, box.at[d], send.at[d], recv.at[d], peer) for d, peer in enumerate(group_peers())]
+
+
+def gathered_sum(part_ref, box):
+    total = part_ref[...]
+    for d in range(box.shape[0]):
+        total = total + box[d]
+    return (adapter_scale * total).astype(bf16)
+
+
+def chain_step(k, first, last, target, inbox, outbox, send, recv, decay, own_ref):
+    copy = remote(outbox.at[k], inbox.at[k], send.at[k], recv.at[k], target)
+
+    @pl.when(first)
+    def _():
+        inbox[k] = jnp.zeros(inbox.shape[1:], f32)
+
+    @pl.when(jnp.logical_not(first))
+    def _():
+        copy.wait_recv()
+
+    @pl.when(jnp.logical_not(last))
+    def _():
+        outbox[k] = decay * inbox[k] + own_ref[CHUNK * k : CHUNK * (k + 1), :]
+        copy.start()
+
+    return copy
+
+
+def start_kernel(part_ref, state_ref, decay_ref, gu_ref, sin_ref, box, inbox, outbox, gsend, grecv, send, recv):
+    ctx = lax.axis_size("ctx")
+    place = lax.axis_index("ctx")
+    first, last = place == 0, place == ctx - 1
+    greet()
+    swaps = exchange(part_ref, box, gsend, grecv)
+    decay = decay_ref[:1, :]
+    target = {"ctx": lax.rem(place + 1, ctx)}
+    copies = []
+    for k in range(inbox.shape[0]):
+        copies.append(chain_step(k, first, last, target, inbox, outbox, send, recv, decay, state_ref))
+        if k == 0:
+            for swap in swaps:
+                swap.start()
+        sin_ref[CHUNK * k : CHUNK * (k + 1), :] = inbox[k]
+    for swap in swaps:
+        swap.wait()
+    gu_ref[...] = gathered_sum(part_ref, box)
+
+    @pl.when(jnp.logical_not(last))
+    def _():
+        for copy in copies:
+            copy.wait_send()
+
+
+def middle_kernel(part_ref, up_ref, gout_ref, ginj_ref, decay_ref, ddown_ref,
+                  gin_ref, out_ref, gdown_ref, gup_ref,
+                  box, inbox, outbox, upbox, sums, downbox,
+                  usend, urecv, send, recv, up_send, up_recv, dn_send, dn_recv):
+    ctx = lax.axis_size("ctx")
+    place = lax.axis_index("ctx")
+    first, last = place == 0, place == ctx - 1
+    chunks = inbox.shape[0]
+    half = chunks // 2
+    above = {"ctx": lax.rem(place + 1, ctx)}
+    below = {"ctx": lax.rem(place + ctx - 1, ctx)}
+    greet()
+    swaps = exchange(part_ref, box, usend, urecv)
+    ups = [remote(sums.at[k], upbox.at[k], up_send.at[k], up_recv.at[k], above) for k in range(chunks)]
+    tops = [remote(sums.at[k], downbox.at[k], dn_send.at[k], dn_recv.at[k], below) for k in range(chunks)]
+    downs = [remote(downbox.at[k], downbox.at[k], dn_send.at[k], dn_recv.at[k], below) for k in range(chunks)]
+    for k in range(half):
+        sums[k] = ddown_ref[CHUNK * k : CHUNK * (k + 1), :]
+
+    def adapter():
+        for swap in swaps:
+            swap.wait()
+        u = gathered_sum(part_ref, box)
+        out_ref[...] = tn(u, up_ref[...]).astype(bf16)
+        dup = nn(u, gout_ref[...])
+        for k in range(half):
+            sums[half + k] = dup[CHUNK * k : CHUNK * (k + 1), :]
+
+    def climb(k):
+        @pl.when(jnp.logical_not(first))
+        def _():
+            ups[k].wait_recv()
+            sums[k] = sums[k] + upbox[k]
+
+            @pl.when(jnp.logical_not(last))
+            def _():
+                ups[k].start()
+
+            @pl.when(last)
+            def _():
+                tops[k].start()
+
+    @pl.when(last)
+    def _():
+        for k in range(chunks):
+            outbox[k] = ginj_ref[CHUNK * k : CHUNK * (k + 1), :]
+            inbox[k] = jnp.zeros(inbox.shape[1:], f32)
+            remote(outbox.at[k], inbox.at[k], send.at[k], recv.at[k], below).start()
+
+    for swap in swaps:
+        swap.start()
+
+    @pl.when(first)
+    def _():
+        for k in range(half):
+            ups[k].start()
+        adapter()
+        for k in range(half, chunks):
+            ups[k].start()
+
+    decay = decay_ref[:1, :]
+    copies = [remote(outbox.at[k], inbox.at[k], send.at[k], recv.at[k], below) for k in range(chunks)]
+    for k in range(chunks):
+
+        @pl.when(jnp.logical_not(last))
+        def _():
+            copies[k].wait_recv()
+
+            @pl.when(jnp.logical_not(first))
+            def _():
+                outbox[k] = decay * inbox[k] + ginj_ref[CHUNK * k : CHUNK * (k + 1), :]
+                copies[k].start()
+
+        if k >= half:
+            climb(k - half)
+        gin_ref[CHUNK * k : CHUNK * (k + 1), :] = inbox[k]
+
+    @pl.when(jnp.logical_not(first))
+    def _():
+        adapter()
+
+    for k in range(half, chunks):
+        climb(k)
+
+    for k in range(chunks):
+
+        @pl.when(jnp.logical_not(last))
+        def _():
+            downs[k].wait_recv()
+            sums_k = downbox[k]
+
+            @pl.when(jnp.logical_not(first))
+            def _():
+                downs[k].start()
+                ups[k].wait_send()
+
+            @pl.when(first)
+            def _():
+                ups[k].wait_send()
+
+            sums[k] = sums_k
+
+    gup_ref[...] = jnp.concatenate([sums[half + k] for k in range(half)], axis=0)
+    gdown_ref[...] = jnp.concatenate([sums[k] for k in range(half)], axis=0).T
+
+    @pl.when(jnp.logical_not(first))
+    def _():
+        for k in range(chunks):
+            copies[k].wait_send()
+            downs[k].wait_send()
+
+
+def call(kernel, name, outs, args, scratch=(), collective_id=None):
+    params = {} if collective_id is None else dict(collective_id=collective_id, has_side_effects=True)
+    whole = pl.BlockSpec(memory_space=pltpu.VMEM)
     return pl.pallas_call(
         kernel,
         name=name,
         out_shape=[jax.ShapeDtypeStruct(s, d) for s, d in outs],
-        in_specs=specs,
-        out_specs=[vm()] * len(outs),
-        compiler_params=pltpu.CompilerParams(vmem_limit_bytes=56 << 20),
+        in_specs=[whole] * len(args),
+        out_specs=[whole] * len(outs),
+        scratch_shapes=list(scratch),
+        compiler_params=pltpu.CompilerParams(vmem_limit_bytes=56 << 20, **params),
     )(*args)
 
 
@@ -238,39 +427,46 @@
     rows, channels = x.shape
     heads = dtin.shape[0]
     rank = down.shape[1]
-    ctx = lax.axis_size("ctx")
-    place = lax.axis_index("ctx").astype(jnp.int32).reshape(1)
     head_dim = channels // heads
-    wide = STATE + 8
-    gu_part = nt(gout, up)
-    gu = (adapter_scale * lax.psum(gu_part, ("head", "fsdp"))).astype(bf16)
+    peers = lax.axis_size("head") * lax.axis_size("fsdp") - 1
+    chunks = STATE // CHUNK
+    assert 2 * rank == STATE
+    dma = pltpu.SemaphoreType.DMA
+    slab = pltpu.VMEM((chunks, CHUNK, channels), f32)
+    swap = pltpu.VMEM((peers, rank, rows), f32)
     skip_row = jnp.repeat(skip, head_dim)[None, :]
     gain_row = gain[None, :]
     rate_row = jnp.pad(rate, (0, LANES - heads))[None, :]
-    e, einv, dt, rc, rr, em, state = call(
+    down_rows = down.T
+    e, einv, dt, rc, rr, em, decay, state = call(
         scan_kernel, "scan",
-        [((rows, LANES), f32)] * 4 + [((8, rows), f32), ((8, channels), f32), ((wide, channels), f32)],
+        [((rows, LANES), f32)] * 4 + [((8, rows), f32), ((8, channels), f32), ((8, channels), f32), ((STATE, channels), f32)],
         (x, b, dtin, bias[:, None], rate[:, None], resets[None, :]),
     )
-    gathered = lax.all_gather(state, "ctx")
-    mixed, dz, gy, gd, sin, ginj, pn, kk, ddown, u_part = call(
-        lambda *r: forward_kernel(ctx, heads, *r), "forward",
+    gu_part = nt(up, gout)
+    gu, sin = call(
+        start_kernel, "start", [((rank, rows), bf16), ((STATE, channels), f32)], (gu_part, state, decay),
+        [swap, slab, slab, dma((peers,)), dma((peers,)), dma((chunks,)), dma((chunks,))], 1,
+    )
+    mixed, dz, gy, gd, ginj, pn, kk, ddown, u_part = call(
+        lambda *r: forward_kernel(heads, *r), "forward",
         [((rows, channels), bf16), ((rows, channels), bf16), ((rows, channels), f32), ((rows, channels), bf16),
-         ((STATE, channels), f32), ((wide, channels), f32), ((rows, LANES), f32), ((8, LANES), f32),
-         ((channels, rank), f32), ((rows, rank), f32)],
-        (place, x, z, b, c, gx, e, einv, dt, rc, rr, em, skip_row, gain_row, down, gu, gathered), 1,
-    )
-    back = lax.all_gather(ginj, "ctx")
-    u = (adapter_scale * lax.psum(u_part, ("head", "fsdp"))).astype(bf16)
-    adapter_output = nn(u, up).astype(bf16)
-    dup = tn(u, gout)
-    ddown, dup = lax.psum((ddown, dup), "ctx")
-    dx, db, dc, dstep, _ = call(
-        lambda *r: backward_kernel(ctx, heads, *r), "backward",
-        [((rows, channels), bf16), (b.shape, bf16), (c.shape, bf16), ((heads, rows), f32), ((STATE, channels), f32)],
-        (place, x, b, c, e, einv, dt, rc, rr, em, skip_row, rate_row, gy, gd, sin, pn, kk, back), 1,
-    )
-    return mixed, adapter_output, dx, dz, db, dc, dstep, ddown, dup
+         ((STATE, channels), f32), ((rows, LANES), f32), ((8, LANES), f32),
+         ((rank, channels), f32), ((rank, rows), f32)],
+        (x, z, b, c, gx, e, einv, dt, rc, rr, em, skip_row, gain_row, down_rows, gu, sin),
+    )
+    gin, adapter_output, gdown, gup = call(
+        middle_kernel, "middle",
+        [((STATE, channels), f32), ((rows, channels), bf16), ((channels, rank), f32), ((rank, channels), f32)],
+        (u_part, up, gout, ginj, decay, ddown),
+        [swap] + [slab] * 5 + [dma((peers,))] * 2 + [dma((chunks,))] * 6, 2,
+    )
+    dx, db, dc, dstep = call(
+        lambda *r: backward_kernel(heads, *r), "backward",
+        [((rows, channels), bf16), (b.shape, bf16), (c.shape, bf16), ((heads, rows), f32)],
+        (x, b, c, e, einv, dt, rc, rr, em, skip_row, rate_row, gy, gd, sin, pn, kk, gin, decay),
+    )
+    return mixed, adapter_output, dx, dz, db, dc, dstep, gdown, gup
 
 
 def solution(mesh):

time: 229 us -> 121 us (0.53)
  waiting for transfers between devices: 167 us -> 0 us
  Pallas kernels: 29.6 us -> 109 us
  between operations: 15.8 us -> 0.69 us
  matrix products: 5.46 us -> 2.4 us
    psum x3 -> x0, waiting for transfers between devices: 97.9 us -> none  [the longest x1 41.5 us: per_device(): ddown, dup = lax.psum((ddown, dup), 'ctx')]
    pallas_call x3 -> x5, Pallas kernels: 29.6 us -> 109 us  [call(): pl.pallas_call(kernel, name=name, out_shape=[jax.ShapeDtypeStruct(s, d) f...]
    all_gather x2 -> x0, waiting for transfers between devices: 69 us -> none  [the longest x1 47.1 us: per_device(): back = lax.all_gather(ginj, 'ctx')]
    dot_general x2 -> x0, matrix products: 3.43 us -> none  [the longest x1 2.05 us: tn(): lax.dot_general(a, b, (((0,), (0,)), ((), ())), preferred_element_type=f32)]
    unnamed x17 -> x9, local copies, waits for them, and re-layouts: 4.66 us -> 2.57 us
  transfers between devices with their start and end apart: 5 -> 0, of which waited for: 5 -> 0; matrix products, arithmetic and copies ran while one was open for 4% -> 0% of each run, Pallas kernels for 2% -> 0%
where the time goes in v1:
time: 121 us; the launch traced here: 120 us
  Pallas kernels  109 us (90%)
  local copies, waits for them, and re-layouts  7.81 us (6%)
  matrix products  2.4 us (2%)
    pallas_call x5, Pallas kernels, call(): pl.pallas_call(kernel, name=name, out_shape=[jax.ShapeDtypeStruct(s, d) f...  109 us
    unnamed x9, local copies, waits for them, and re-layouts  2.57 us

profile of v1, /device:TPU:0, one launch (start us, length us, event | category | flops | bytes accessed | tf_op | source)
XLA Modules:
  0.0 120.3 jit_solution(2815580517753387214)
XLA Ops:
  0.6 1.2 pad_bitcast_fusion.r_10_
  1.8 1.3 %copy.23.bias_ref = f32[16,1]{1,0:T(8,128)} copy(f32[16,1]{0,1:T(1,128)} %bitcast.12) | data formatting | bytes 128 | tf_op jit(solution)/shard_map/broadcast_in_dim | solution.py:444
  3.2 0.7 broadcast_in_dim.21
  3.9 0.7 broadcast_in_dim_reshape.3.r_11_.r_9_
  4.6 1.3 %copy.24.rate_ref = f32[16,1]{1,0:T(8,128)} copy(f32[16,1]{0,1:T(1,128)} %bitcast.13) | data formatting | bytes 128 | tf_op jit(solution)/shard_map/broadcast_in_dim | solution.py:444
  5.9 2.4 %fusion.part_ref = f32[64,512]{1,0:T(8,128)} fusion(bf16[64,1024]{1,0:T(8,128)(2,1)} %up_ref.1, bf16[512,1024]{1,0:T(8,128)(2,1)} %gout_ref.1), kind=kOutput, calls=%fused_computation.1 | convolution fusion | flops 67108864 | bytes 1310720 | tf_op jit(solution)/shard_map/dot_general | solution.py:22
  8.3 5.6 %scan.1 = (f32[512,128]{1,0:T(8,128)}, f32[512,128]{1,0:T(8,128)}, f32[512,128]{1,0:T(8,128)}, f32[512,128]{1,0:T(8,128)}, f32[8,512]{1,0:T(8,128)}, /*index=5*/...) custom-call(bf16[512,1024]{1,0:T(8,128)(2,1)} %r_0_.3, bf16[512,256]{1,0:T(8,128)(2,1)} %r_1_.3, ...), custom_call_target="tpu_custom_call" | custom-call | tf_op jit(solution)/shard_map/scan/pallas_call | solution.py:415
  13.9 16.8 %start.1 = (bf16[64,512]{1,0:T(8,128)(2,1)}, f32[128,1024]{1,0:T(8,128)}) custom-call(f32[64,512]{1,0:T(8,128)} %fusion.part_ref, f32[128,1024]{1,0:T(8,128)} %get-tuple-element.42.state_ref, f32[8,1024]{1,0:T(8,128)} %get-tuple-element.43.decay_ref.r_17_), custom_call_target="tpu_custom_call" | custom-call | tf_op jit(solution)/shard_map/start/pallas_call | solution.py:415
  30.7 10.8 %forward.1 = (bf16[512,1024]{1,0:T(8,128)(2,1)}, bf16[512,1024]{1,0:T(8,128)(2,1)}, f32[512,1024]{1,0:T(8,128)}, bf16[512,1024]{1,0:T(8,128)(2,1)}, f32[128,1024...) custom-call(bf16[512,1024]{1,0:T(8,128)(2,1)} %r_0_.3, ...), custom_call_target="tpu_custom_call" | custom-call | tf_op jit(solution)/shard_map/forward/pallas_call | solution.py:415
  41.4 65.4 %middle.1 = (f32[128,1024]{1,0:T(8,128)}, bf16[512,1024]{1,0:T(8,128)(2,1)}, f32[1024,64]{1,0:T(8,128)}, f32[64,1024]{1,0:T(8,128)}) custom-call(f32[64,512]{1,0:T(8,128)} %get-tuple-element.47.part_ref, bf16[64,1024]{1,0:T(8,128)(2,1)} %up_ref.1, bf16[512,1024]{1,0:T(8,128)(2,1)} %gout_ref.1, f32[128,1024]{1,0:T(8,128)} %get-tuple-element.48.ginj_ref, ...), custom_call_target="tpu_custom_call" | custom-call | tf_op jit(solution)/shard_map/middle/pallas_call | solution.py:415
  106.9 0.0 copy-start.1
  106.9 0.0 copy-start
  106.9 10.8 %backward.1 = (bf16[512,1024]{1,0:T(8,128)(2,1)}, bf16[512,256]{1,0:T(8,128)(2,1)}, bf16[512,256]{1,0:T(8,128)(2,1)}, f32[16,512]{1,0:T(8,128)}) custom-call(bf16[512,1024]{1,0:T(8,128)(2,1)} %r_0_.3, bf16[512,256]{1,0:T(8,128)(2,1)} %r_1_.3, bf16[512,256]{1,0:T(8,128)(2,1)} %r_2_.3, f32[512,128]{1,0:T(8,128)} %get-tuple-element.36.r_5_.r_3_, ...), custom_call_target="tpu_custom_call" | custom-call | tf_op jit(solution)/shard_map/backward/pallas_call | solution.py:415
  117.7 0.0 copy-start.2
  117.7 0.0 copy-done.1
  117.7 0.9 copy.25
  118.6 0.0 copy-done
  118.6 1.0 copy.28
  119.6 0.0 copy-done.2
  119.6 0.7 copy.29
Async XLA Ops:
  106.9 10.9 %copy-start.1 = (f32[1024,64]{1,0:T(8,128)S(1)}, f32[1024,64]{1,0:T(8,128)}, u32[]{:S(2)}) copy-start(f32[1024,64]{1,0:T(8,128)} %get-tuple-element.70) | copy-start | bytes 786436
  106.9 11.7 %copy-start = (bf16[512,1024]{1,0:T(8,128)(2,1)S(1)}, bf16[512,1024]{1,0:T(8,128)(2,1)}, u32[]{:S(2)}) copy-start(bf16[512,1024]{1,0:T(8,128)(2,1)} %get-tuple-element.82) | copy-start | bytes 3145732
  117.7 1.9 %copy-start.2 = (f32[64,1024]{1,0:T(8,128)S(1)}, f32[64,1024]{1,0:T(8,128)}, u32[]{:S(2)}) copy-start(f32[64,1024]{1,0:T(8,128)} %get-tuple-element.89) | copy-start | bytes 786436

commit v2 on v1

--- a/solution.py
+++ b/solution.py
@@ -50,6 +50,18 @@
     return nn(hi, pick) + nn(lo, pick)
 
 
+def padded(row):
+    return jnp.concatenate([row, jnp.zeros((1, LANES - row.shape[1]), f32)], axis=1)
+
+
+def tall(row):
+    return jnp.broadcast_to(padded(row), (LANES, LANES)).T[: row.shape[1], :1]
+
+
+def wide_row(row, group, per_group, width):
+    return expand(jnp.broadcast_to(padded(row), (8, LANES)), group, per_group, width)[:1]
+
+
 def score_mask(rid_col, rid_row):
     n = rid_col.shape[0]
     return (rid_col == rid_row) & (iota((n, n), 0) >= iota((n, n), 1))
@@ -62,9 +74,9 @@
     groups = b_ref.shape[1] // STATE
     per_group = heads // groups
     width = x_ref.shape[1] // groups
-    v = dtin_ref[...] + bias_ref[...]
+    v = dtin_ref[...] + tall(bias_ref[...])
     dt = jnp.maximum(v, 0.0) + jnp.log1p(jnp.exp(-jnp.abs(v)))
-    log_step = -rate_ref[...] * dt
+    log_step = -tall(rate_ref[...]) * dt
     marks = jnp.broadcast_to(resets_ref[...].astype(f32), (8, rows))
     stack = jnp.concatenate([log_step, marks, jnp.zeros((LANES - heads - 8, rows), f32)], axis=0)
     dt_cols = jnp.concatenate([dt, jnp.zeros((LANES - heads, rows), f32)], axis=0).T
@@ -122,7 +134,7 @@
         em = em_ref[:1, cols]
         s = (em * sin_ref[:, cols]).astype(bf16)
         inner = nn(a, xd) + nn(c0, s)
-        y = ex * inner + skip_ref[:, cols] * x
+        y = ex * inner + wide_row(skip_ref[...], g, per_group, width) * x
         z = z_ref[:, cols].astype(f32)
         sig = 1.0 / (1.0 + jnp.exp(-z))
         act = z * sig
@@ -152,12 +164,34 @@
 
 
 def backward_kernel(heads, x_ref, b_ref, c_ref, e_ref, einv_ref, dt_ref, rc_ref, rr_ref, em_ref,
-                    skip_ref, rate_ref, gy_ref, gd_ref, sin_ref, pn_ref, k_ref, gin_ref, decay_ref,
-                    dx_ref, db_ref, dc_ref, dstep_ref):
+                    skip_ref, rate_ref, gy_ref, gd_ref, sin_ref, pn_ref, k_ref, gin_ref, decay_ref, ddown_ref, dup_ref,
+                    dx_ref, db_ref, dc_ref, dstep_ref, gdown_ref, gup_ref,
+                    mine, arrived, totals, send, recv, back_send, back_recv):
     rows = x_ref.shape[0]
     groups = b_ref.shape[1] // STATE
     width = x_ref.shape[1] // groups
     per_group = heads // groups
+    ctx = lax.axis_size("ctx")
+    place = lax.axis_index("ctx")
+    share = mine.shape[1]
+    rank = ddown_ref.shape[0]
+    others = [lax.rem(place + d, ctx) for d in range(1, ctx)]
+    barrier = pltpu.get_barrier_semaphore()
+    for other in others:
+        pl.semaphore_signal(barrier, inc=1, device_id={"ctx": other}, device_id_type=pl.DeviceIdType.MESH)
+    for j in range(ctx):
+        lo = j * share
+        mine[j] = ddown_ref[lo : lo + share, :] if lo < rank else dup_ref[lo - rank : lo - rank + share, :]
+    pl.semaphore_wait(barrier, ctx - 1)
+    out_copies = [
+        remote(mine.at[j], arrived.at[d], send.at[d], recv.at[d], {"ctx": j}) for d, j in enumerate(others)
+    ]
+    back_copies = [
+        remote(totals.at[place], totals.at[place], back_send.at[d], back_recv.at[d], {"ctx": j})
+        for d, j in enumerate(others)
+    ]
+    for copy in out_copies:
+        copy.start()
     mask = score_mask(rc_ref[:, :1], rr_ref[:1, :])
     fresh = rc_ref[:, :1] == 0
     ends = rc_ref[:, :1] == rc_ref[rows - 1 : rows, :1]
@@ -182,7 +216,7 @@
         s = (em * sin).astype(bf16)
         ge = (em * gin).astype(bf16)
         v = tn(a, gd) + nn(b_end, ge)
-        dx_ref[:, cols] = (fx * v + skip_ref[:, cols] * gy_ref[:, cols]).astype(bf16)
+        dx_ref[:, cols] = (fx * v + wide_row(skip_ref[...], g, per_group, width) * gy_ref[:, cols]).astype(bf16)
         pair = jnp.where(mask, nt(gd, xd), 0.0).astype(bf16)
         dc_ref[:, narrow] = (nn(pair, b) + jnp.where(fresh, nt(gd, s), 0.0)).astype(bf16)
         db_ref[:, narrow] = (tn(pair, c) + jnp.where(ends, nt(xd, ge), 0.0)).astype(bf16)
@@ -190,11 +224,23 @@
         step = step + headsum(x * v, g, per_group)
         through = decay_ref[:1, cols] * jnp.sum(sin * gin, axis=0, keepdims=True)
         kk = kk + headsum(jnp.broadcast_to(through, (8, width)), g, per_group)
+        if g == 0:
+            total = mine[place]
+            for d, copy in enumerate(out_copies):
+                copy.wait()
+                total = total + arrived[d]
+            totals[place] = total
+            for copy in back_copies:
+                copy.start()
     before = jnp.where(iota((rows, rows), 0) > iota((rows, rows), 1), 1.0, 0.0)
     glog = lax.dot_general(before, net, (((1,), (0,)), ((), ())), precision=highest, preferred_element_type=f32) + kk[:1]
-    gdt = einv_ref[...] * step - rate_ref[...] * glog
+    gdt = einv_ref[...] * step - padded(rate_ref[...]) * glog
     out = gdt * (1.0 - jnp.exp(-dt_ref[...]))
     dstep_ref[...] = out.T[: dstep_ref.shape[0], :]
+    for copy in back_copies:
+        copy.wait()
+    gdown_ref[...] = jnp.concatenate([totals[j] for j in range(ctx // 2)], axis=0).T
+    gup_ref[...] = jnp.concatenate([totals[j] for j in range(ctx // 2, ctx)], axis=0)
 
 
 CHUNK = 16
@@ -297,72 +343,43 @@
             copy.wait_send()
 
 
-def middle_kernel(part_ref, up_ref, gout_ref, ginj_ref, decay_ref, ddown_ref,
-                  gin_ref, out_ref, gdown_ref, gup_ref,
-                  box, inbox, outbox, upbox, sums, downbox,
-                  usend, urecv, send, recv, up_send, up_recv, dn_send, dn_recv):
+def middle_kernel(part_ref, up_ref, gout_ref, ginj_ref, decay_ref, gin_ref, out_ref, dup_ref,
+                  box, inbox, outbox, usend, urecv, send, recv):
     ctx = lax.axis_size("ctx")
     place = lax.axis_index("ctx")
     first, last = place == 0, place == ctx - 1
     chunks = inbox.shape[0]
-    half = chunks // 2
-    above = {"ctx": lax.rem(place + 1, ctx)}
     below = {"ctx": lax.rem(place + ctx - 1, ctx)}
     greet()
     swaps = exchange(part_ref, box, usend, urecv)
-    ups = [remote(sums.at[k], upbox.at[k], up_send.at[k], up_recv.at[k], above) for k in range(chunks)]
-    tops = [remote(sums.at[k], downbox.at[k], dn_send.at[k], dn_recv.at[k], below) for k in range(chunks)]
-    downs = [remote(downbox.at[k], downbox.at[k], dn_send.at[k], dn_recv.at[k], below) for k in range(chunks)]
-    for k in range(half):
-        sums[k] = ddown_ref[CHUNK * k : CHUNK * (k + 1), :]
+    copies = [remote(outbox.at[k], inbox.at[k], send.at[k], recv.at[k], below) for k in range(chunks)]
 
     def adapter():
         for swap in swaps:
             swap.wait()
         u = gathered_sum(part_ref, box)
         out_ref[...] = tn(u, up_ref[...]).astype(bf16)
-        dup = nn(u, gout_ref[...])
-        for k in range(half):
-            sums[half + k] = dup[CHUNK * k : CHUNK * (k + 1), :]
-
-    def climb(k):
-        @pl.when(jnp.logical_not(first))
-        def _():
-            ups[k].wait_recv()
-            sums[k] = sums[k] + upbox[k]
-
-            @pl.when(jnp.logical_not(last))
-            def _():
-                ups[k].start()
-
-            @pl.when(last)
-            def _():
-                tops[k].start()
+        dup_ref[...] = nn(u, gout_ref[...])
 
     @pl.when(last)
     def _():
         for k in range(chunks):
             outbox[k] = ginj_ref[CHUNK * k : CHUNK * (k + 1), :]
-            inbox[k] = jnp.zeros(inbox.shape[1:], f32)
-            remote(outbox.at[k], inbox.at[k], send.at[k], recv.at[k], below).start()
+            copies[k].start()
+        gin_ref[...] = jnp.zeros_like(gin_ref)
 
     for swap in swaps:
         swap.start()
 
     @pl.when(first)
     def _():
-        for k in range(half):
-            ups[k].start()
         adapter()
-        for k in range(half, chunks):
-            ups[k].start()
 
     decay = decay_ref[:1, :]
-    copies = [remote(outbox.at[k], inbox.at[k], send.at[k], recv.at[k], below) for k in range(chunks)]
-    for k in range(chunks):
-
-        @pl.when(jnp.logical_not(last))
-        def _():
+
+    @pl.when(jnp.logical_not(last))
+    def _():
+        for k in range(chunks):
             copies[k].wait_recv()
 
             @pl.when(jnp.logical_not(first))
@@ -370,43 +387,13 @@
                 outbox[k] = decay * inbox[k] + ginj_ref[CHUNK * k : CHUNK * (k + 1), :]
                 copies[k].start()
 
-        if k >= half:
-            climb(k - half)
-        gin_ref[CHUNK * k : CHUNK * (k + 1), :] = inbox[k]
+            gin_ref[CHUNK * k : CHUNK * (k + 1), :] = inbox[k]
 
     @pl.when(jnp.logical_not(first))
     def _():
         adapter()
-
-    for k in range(half, chunks):
-        climb(k)
-
-    for k in range(chunks):
-
-        @pl.when(jnp.logical_not(last))
-        def _():
-            downs[k].wait_recv()
-            sums_k = downbox[k]
-
-            @pl.when(jnp.logical_not(first))
-            def _():
-                downs[k].start()
-                ups[k].wait_send()
-
-            @pl.when(first)
-            def _():
-                ups[k].wait_send()
-
-            sums[k] = sums_k
-
-    gup_ref[...] = jnp.concatenate([sums[half + k] for k in range(half)], axis=0)
-    gdown_ref[...] = jnp.concatenate([sums[k] for k in range(half)], axis=0).T
-
-    @pl.when(jnp.logical_not(first))
-    def _():
         for k in range(chunks):
             copies[k].wait_send()
-            downs[k].wait_send()
 
 
 def call(kernel, name, outs, args, scratch=(), collective_id=None):
@@ -427,21 +414,20 @@
     rows, channels = x.shape
     heads = dtin.shape[0]
     rank = down.shape[1]
-    head_dim = channels // heads
     peers = lax.axis_size("head") * lax.axis_size("fsdp") - 1
     chunks = STATE // CHUNK
     assert 2 * rank == STATE
     dma = pltpu.SemaphoreType.DMA
     slab = pltpu.VMEM((chunks, CHUNK, channels), f32)
     swap = pltpu.VMEM((peers, rank, rows), f32)
-    skip_row = jnp.repeat(skip, head_dim)[None, :]
+    skip_row = skip[None, :]
     gain_row = gain[None, :]
-    rate_row = jnp.pad(rate, (0, LANES - heads))[None, :]
+    rate_row = rate[None, :]
     down_rows = down.T
     e, einv, dt, rc, rr, em, decay, state = call(
         scan_kernel, "scan",
         [((rows, LANES), f32)] * 4 + [((8, rows), f32), ((8, channels), f32), ((8, channels), f32), ((STATE, channels), f32)],
-        (x, b, dtin, bias[:, None], rate[:, None], resets[None, :]),
+        (x, b, dtin, bias[None, :], rate_row, resets[None, :]),
     )
     gu_part = nt(up, gout)
     gu, sin = call(
@@ -455,16 +441,21 @@
          ((rank, channels), f32), ((rank, rows), f32)],
         (x, z, b, c, gx, e, einv, dt, rc, rr, em, skip_row, gain_row, down_rows, gu, sin),
     )
-    gin, adapter_output, gdown, gup = call(
+    gin, adapter_output, dup = call(
         middle_kernel, "middle",
-        [((STATE, channels), f32), ((rows, channels), bf16), ((channels, rank), f32), ((rank, channels), f32)],
-        (u_part, up, gout, ginj, decay, ddown),
-        [swap] + [slab] * 5 + [dma((peers,))] * 2 + [dma((chunks,))] * 6, 2,
-    )
-    dx, db, dc, dstep = call(
+        [((STATE, channels), f32), ((rows, channels), bf16), ((rank, channels), f32)],
+        (u_part, up, gout, ginj, decay),
+        [swap, slab, slab] + [dma((peers,))] * 2 + [dma((chunks,))] * 2, 2,
+    )
+    ctx = lax.axis_size("ctx")
+    share = STATE // ctx
+    dx, db, dc, dstep, gdown, gup = call(
         lambda *r: backward_kernel(heads, *r), "backward",
-        [((rows, channels), bf16), (b.shape, bf16), (c.shape, bf16), ((heads, rows), f32)],
-        (x, b, c, e, einv, dt, rc, rr, em, skip_row, rate_row, gy, gd, sin, pn, kk, gin, decay),
+        [((rows, channels), bf16), (b.shape, bf16), (c.shape, bf16), ((heads, rows), f32),
+         ((channels, rank), f32), ((rank, channels), f32)],
+        (x, b, c, e, einv, dt, rc, rr, em, skip_row, rate_row, gy, gd, sin, pn, kk, gin, decay, ddown, dup),
+        [pltpu.VMEM((ctx, share, channels), f32), pltpu.VMEM((ctx - 1, share, channels), f32),
+         pltpu.VMEM((ctx, share, channels), f32)] + [dma((ctx - 1,))] * 4, 3,
     )
     return mixed, adapter_output, dx, dz, db, dc, dstep, gdown, gup
 

time: 121 us -> 104 us (0.86)
  Pallas kernels: 109 us -> 94.2 us
    pallas_call x5, Pallas kernels: 109 us -> 94.2 us  [call(): pl.pallas_call(kernel, name=name, out_shape=[jax.ShapeDtypeStruct(s, d) f...]
    broadcast_in_dim x4 -> x0, local copies, waits for them, and re-layouts: 4.58 us -> none  [the longest x1 1.33 us: per_device(): bias[:, None]]
    unnamed x9 -> x19, local copies, waits for them, and re-layouts: 2.57 us -> 6.7 us
where the time goes in v2:
time: 104 us
  Pallas kernels  94.2 us (91%)
  local copies, waits for them, and re-layouts  6.7 us (6%)
  matrix products  2.4 us (2%)
    pallas_call x5, Pallas kernels, call(): pl.pallas_call(kernel, name=name, out_shape=[jax.ShapeDtypeStruct(s, d) f...  94.2 us
    unnamed x19, local copies, waits for them, and re-layouts  6.7 us
    dot_general x1, matrix products, nt(): lax.dot_general(a, b, (((1,), (1,)), ((), ())), preferred_element_type=f32)  2.4 us

profile of v2, /device:TPU:0, one launch (start us, length us, event | category | flops | bytes accessed | tf_op | source)
XLA Modules:
  0.0 104.0 jit_solution(18217512591518835056)
XLA Ops:
  0.6 2.4 %fusion.part_ref = f32[64,512]{1,0:T(8,128)} fusion(bf16[64,1024]{1,0:T(8,128)(2,1)} %up_ref.1, bf16[512,1024]{1,0:T(8,128)(2,1)} %gout_ref.1), kind=kOutput, calls=%fused_computation | convolution fusion | flops 67108864 | bytes 1310720 | tf_op jit(solution)/shard_map/dot_general | solution.py:22
  3.0 5.7 %scan.1 = (f32[512,128]{1,0:T(8,128)}, f32[512,128]{1,0:T(8,128)}, f32[512,128]{1,0:T(8,128)}, f32[512,128]{1,0:T(8,128)}, f32[8,512]{1,0:T(8,128)}, /*index=5*/...) custom-call(bf16[512,1024]{1,0:T(8,128)(2,1)} %r_0_.3, bf16[512,256]{1,0:T(8,128)(2,1)} %r_1_.3, ...), custom_call_target="tpu_custom_call" | custom-call | tf_op jit(solution)/shard_map/scan/pallas_call | solution.py:402
  8.7 16.8 %start.1 = (bf16[64,512]{1,0:T(8,128)(2,1)}, f32[128,1024]{1,0:T(8,128)}) custom-call(f32[64,512]{1,0:T(8,128)} %fusion.part_ref, f32[128,1024]{1,0:T(8,128)} %get-tuple-element.43.state_ref, f32[8,1024]{1,0:T(8,128)} %get-tuple-element.44.decay_ref.r_17_), custom_call_target="tpu_custom_call" | custom-call | tf_op jit(solution)/shard_map/start/pallas_call | solution.py:402
  25.5 11.3 %forward.1 = (bf16[512,1024]{1,0:T(8,128)(2,1)}, bf16[512,1024]{1,0:T(8,128)(2,1)}, f32[512,1024]{1,0:T(8,128)}, bf16[512,1024]{1,0:T(8,128)(2,1)}, f32[128,1024...) custom-call(bf16[512,1024]{1,0:T(8,128)(2,1)} %r_0_.3, ...), custom_call_target="tpu_custom_call" | custom-call | tf_op jit(solution)/shard_map/forward/pallas_call | solution.py:402
  36.8 32.6 %middle.1 = (f32[128,1024]{1,0:T(8,128)}, bf16[512,1024]{1,0:T(8,128)(2,1)}, f32[64,1024]{1,0:T(8,128)}) custom-call(f32[64,512]{1,0:T(8,128)} %get-tuple-element.48.part_ref, bf16[64,1024]{1,0:T(8,128)(2,1)} %up_ref.1, bf16[512,1024]{1,0:T(8,128)(2,1)} %gout_ref.1, f32[128,1024]{1,0:T(8,128)} %get-tuple-element.49.ginj_ref, ...), custom_call_target="tpu_custom_call" | custom-call | tf_op jit(solution)/shard_map/middle/pallas_call | solution.py:402
  69.4 0.0 copy-start
  69.4 27.9 %backward.1 = (bf16[512,1024]{1,0:T(8,128)(2,1)}, bf16[512,256]{1,0:T(8,128)(2,1)}, bf16[512,256]{1,0:T(8,128)(2,1)}, f32[16,512]{1,0:T(8,128)}, f32[1024,64]{1,0:T(8,128)}, /*index=5*/f32[64,1024]{1,0:T(8,128)}) custom-call(bf16[512,1024]{1,0:T(8,128)(2,1)} %r_0_.3, bf16[512,256]{1,0:T(8,128)(2,1)} %r_1_.3, bf16[512,256]{1,0:T(8,128)(2,1)} %r_2_.3, ...), custom_call_target="tpu_custom_call" | custom-call | tf_op jit(solution)/shard_map/backward/pallas_call | solution.py:402
  97.2 0.0 copy-start.1
  97.3 2.0 %copy.23 = f32[1024,64]{0,1:T(8,128)} copy(f32[1024,64]{1,0:T(8,128)} %get-tuple-element.72) | data formatting | bytes 524288
  99.3 0.0 copy-done
  99.3 0.0 copy-start.4
  99.3 0.0 copy-start.3
  99.3 1.0 copy.30
  100.2 0.0 copy-done.1
  100.2 0.0 copy-start.5
  100.2 0.0 copy-start.2
  100.3 1.0 copy.31
  101.2 0.0 copy-done.4
  101.2 0.7 copy.32
  101.9 0.0 copy-done.3
  101.9 0.7 copy.33
  102.6 0.0 copy-done.5
  102.6 0.6 copy.34
  103.3 0.0 copy-done.2
  103.3 0.7 copy.35
Async XLA Ops:
  69.4 29.9 %copy-start = (bf16[512,1024]{1,0:T(8,128)(2,1)S(1)}, bf16[512,1024]{1,0:T(8,128)(2,1)}, u32[]{:S(2)}) copy-start(bf16[512,1024]{1,0:T(8,128)(2,1)} %get-tuple-element.84) | copy-start | bytes 3145732
  97.2 3.0 %copy-start.1 = (bf16[512,1024]{1,0:T(8,128)(2,1)S(1)}, bf16[512,1024]{1,0:T(8,128)(2,1)}, u32[]{:S(2)}) copy-start(bf16[512,1024]{1,0:T(8,128)(2,1)} %get-tuple-element.85) | copy-start | bytes 3145732
  99.3 2.0 %copy-start.4 = (bf16[512,256]{1,0:T(8,128)(2,1)S(1)}, bf16[512,256]{1,0:T(8,128)(2,1)}, u32[]{:S(2)}) copy-start(bf16[512,256]{1,0:T(8,128)(2,1)} %get-tuple-element.87) | copy-start | bytes 786436
  99.3 2.7 %copy-start.3 = (bf16[512,256]{1,0:T(8,128)(2,1)S(1)}, bf16[512,256]{1,0:T(8,128)(2,1)}, u32[]{:S(2)}) copy-start(bf16[512,256]{1,0:T(8,128)(2,1)} %get-tuple-element.88) | copy-start | bytes 786436
  100.2 2.4 %copy-start.5 = (f32[16,512]{1,0:T(8,128)S(1)}, f32[16,512]{1,0:T(8,128)}, u32[]{:S(2)}) copy-start(f32[16,512]{1,0:T(8,128)} %get-tuple-element.89) | copy-start | bytes 98308
  100.2 3.0 %copy-start.2 = (f32[64,1024]{1,0:T(8,128)S(1)}, f32[64,1024]{1,0:T(8,128)}, u32[]{:S(2)}) copy-start(f32[64,1024]{1,0:T(8,128)} %get-tuple-element.91) | copy-start | bytes 786436

commit v3 on v2

--- a/solution.py
+++ b/solution.py
@@ -163,10 +163,178 @@
     k_ref[...] = kk
 
 
+CHUNK = 8
+
+
+def remote(src, dst, send, recv, target):
+    return pltpu.make_async_remote_copy(
+        src_ref=src, dst_ref=dst, send_sem=send, recv_sem=recv, device_id=target,
+        device_id_type=pl.DeviceIdType.MESH,
+    )
+
+
+def group_peers():
+    inner = lax.axis_size("fsdp")
+    count = lax.axis_size("head") * inner
+    me = lax.axis_index("head") * inner + lax.axis_index("fsdp")
+    ids = [lax.rem(me + d, count) for d in range(1, count)]
+    return [{"head": lax.div(i, inner), "fsdp": lax.rem(i, inner)} for i in ids]
+
+
+def greet():
+    ctx = lax.axis_size("ctx")
+    place = lax.axis_index("ctx")
+    barrier = pltpu.get_barrier_semaphore()
+    peers = group_peers()
+    for peer in peers:
+        pl.semaphore_signal(barrier, inc=1, device_id=peer, device_id_type=pl.DeviceIdType.MESH)
+
+    @pl.when(place > 0)
+    def _():
+        pl.semaphore_signal(barrier, inc=1, device_id={"ctx": place - 1}, device_id_type=pl.DeviceIdType.MESH)
+
+    @pl.when(place < ctx - 1)
+    def _():
+        pl.semaphore_signal(barrier, inc=1, device_id={"ctx": place + 1}, device_id_type=pl.DeviceIdType.MESH)
+
+    ends = (place == 0) | (place == ctx - 1)
+
+    @pl.when(ends)
+    def _():
+        pl.semaphore_wait(barrier, len(peers) + 1)
+
+    @pl.when(jnp.logical_not(ends))
+    def _():
+        pl.semaphore_wait(barrier, len(peers) + 2)
+
+
+def exchange(part_ref, box, send, recv):
+    return [remote(part_ref, box.at[d], send.at[d], recv.at[d], peer) for d, peer in enumerate(group_peers())]
+
+
+def gathered_sum(part_ref, box):
+    total = part_ref[...]
+    for d in range(box.shape[0]):
+        total = total + box[d]
+    return (adapter_scale * total).astype(bf16)
+
+
+def chain_step(k, first, last, target, inbox, outbox, send, recv, decay, own_ref):
+    copy = remote(outbox.at[k], inbox.at[k], send.at[k], recv.at[k], target)
+
+    @pl.when(first)
+    def _():
+        inbox[k] = jnp.zeros(inbox.shape[1:], f32)
+
+    @pl.when(jnp.logical_not(first))
+    def _():
+        copy.wait_recv()
+
+    @pl.when(jnp.logical_not(last))
+    def _():
+        outbox[k] = decay * inbox[k] + own_ref[CHUNK * k : CHUNK * (k + 1), :]
+        copy.start()
+
+    return copy
+
+
+def start_kernel(part_ref, state_ref, decay_ref, gu_ref, sin_ref, box, inbox, outbox, gsend, grecv, send, recv):
+    ctx = lax.axis_size("ctx")
+    place = lax.axis_index("ctx")
+    first, last = place == 0, place == ctx - 1
+    greet()
+    swaps = exchange(part_ref, box, gsend, grecv)
+    decay = decay_ref[:1, :]
+    target = {"ctx": lax.rem(place + 1, ctx)}
+    copies = []
+    for k in range(inbox.shape[0]):
+        copies.append(chain_step(k, first, last, target, inbox, outbox, send, recv, decay, state_ref))
+        if k == 0:
+            for swap in swaps:
+                swap.start()
+        sin_ref[CHUNK * k : CHUNK * (k + 1), :] = inbox[k]
+    for swap in swaps:
+        swap.wait()
+    gu_ref[...] = gathered_sum(part_ref, box)
+
+    @pl.when(jnp.logical_not(last))
+    def _():
+        for copy in copies:
+            copy.wait_send()
+
+
+def greet_all():
+    ctx = lax.axis_size("ctx")
+    place = lax.axis_index("ctx")
+    barrier = pltpu.get_barrier_semaphore()
+    peers = group_peers() + [{"ctx": lax.rem(place + d, ctx)} for d in range(1, ctx)]
+    for peer in peers:
+        pl.semaphore_signal(barrier, inc=1, device_id=peer, device_id_type=pl.DeviceIdType.MESH)
+    pl.semaphore_wait(barrier, len(peers))
+
+
+def middle_part(reduce_start, part_ref, up_ref, gout_ref, ginj_ref, decay_ref, gin_ref, out_ref,
+                box, inbox, outbox, usend, urecv, send, recv):
+    ctx = lax.axis_size("ctx")
+    place = lax.axis_index("ctx")
+    first, last = place == 0, place == ctx - 1
+    chunks = inbox.shape[0]
+    below = {"ctx": lax.rem(place + ctx - 1, ctx)}
+    greet_all()
+    swaps = exchange(part_ref, box, usend, urecv)
+    copies = [remote(outbox.at[k], inbox.at[k], send.at[k], recv.at[k], below) for k in range(chunks)]
+
+    def adapter():
+        for swap in swaps:
+            swap.wait()
+        u = gathered_sum(part_ref, box)
+        out_ref[...] = tn(u, up_ref[...]).astype(bf16)
+        reduce_start(nn(u, gout_ref[...]))
+
+    @pl.when(last)
+    def _():
+        for k in range(chunks):
+            outbox[k] = ginj_ref[CHUNK * k : CHUNK * (k + 1), :]
+            copies[k].start()
+        gin_ref[...] = jnp.zeros_like(gin_ref)
+
+    for swap in swaps:
+        swap.start()
+
+    early = place * 2 < ctx
+
+    @pl.when(early)
+    def _():
+        adapter()
+
+    decay = decay_ref[:1, :]
+
+    @pl.when(jnp.logical_not(last))
+    def _():
+        for k in range(chunks):
+            copies[k].wait_recv()
+
+            @pl.when(jnp.logical_not(first))
+            def _():
+                outbox[k] = decay * inbox[k] + ginj_ref[CHUNK * k : CHUNK * (k + 1), :]
+                copies[k].start()
+
+            gin_ref[CHUNK * k : CHUNK * (k + 1), :] = inbox[k]
+
+    @pl.when(jnp.logical_not(early))
+    def _():
+        adapter()
+
+    @pl.when(jnp.logical_not(first))
+    def _():
+        for k in range(chunks):
+            copies[k].wait_send()
+
+
 def backward_kernel(heads, x_ref, b_ref, c_ref, e_ref, einv_ref, dt_ref, rc_ref, rr_ref, em_ref,
-                    skip_ref, rate_ref, gy_ref, gd_ref, sin_ref, pn_ref, k_ref, gin_ref, decay_ref, ddown_ref, dup_ref,
-                    dx_ref, db_ref, dc_ref, dstep_ref, gdown_ref, gup_ref,
-                    mine, arrived, totals, send, recv, back_send, back_recv):
+                    skip_ref, rate_ref, gy_ref, gd_ref, sin_ref, pn_ref, k_ref, decay_ref, ddown_ref, part_ref, up_ref, gout_ref, ginj_ref,
+                    dx_ref, db_ref, dc_ref, dstep_ref, gdown_ref, gup_ref, out_ref,
+                    gin_ref, box, inbox, outbox, usend, urecv, chain_send, chain_recv, mine, arrived, totals, send, recv, back_send, back_recv):
     rows = x_ref.shape[0]
     groups = b_ref.shape[1] // STATE
     width = x_ref.shape[1] // groups
@@ -176,13 +344,6 @@
     share = mine.shape[1]
     rank = ddown_ref.shape[0]
     others = [lax.rem(place + d, ctx) for d in range(1, ctx)]
-    barrier = pltpu.get_barrier_semaphore()
-    for other in others:
-        pl.semaphore_signal(barrier, inc=1, device_id={"ctx": other}, device_id_type=pl.DeviceIdType.MESH)
-    for j in range(ctx):
-        lo = j * share
-        mine[j] = ddown_ref[lo : lo + share, :] if lo < rank else dup_ref[lo - rank : lo - rank + share, :]
-    pl.semaphore_wait(barrier, ctx - 1)
     out_copies = [
         remote(mine.at[j], arrived.at[d], send.at[d], recv.at[d], {"ctx": j}) for d, j in enumerate(others)
     ]
@@ -190,7 +351,22 @@
         remote(totals.at[place], totals.at[place], back_send.at[d], back_recv.at[d], {"ctx": j})
         for d, j in enumerate(others)
     ]
-    for copy in out_copies:
+
+    def reduce_start(dup):
+        for j in range(ctx):
+            lo = j * share
+            mine[j] = ddown_ref[lo : lo + share, :] if lo < rank else dup[lo - rank : lo - rank + share, :]
+        for copy in out_copies:
+            copy.start()
+
+    middle_part(reduce_start, part_ref, up_ref, gout_ref, ginj_ref, decay_ref, gin_ref, out_ref,
+                box, inbox, outbox, usend, urecv, chain_send, chain_recv)
+    total = mine[place]
+    for d, copy in enumerate(out_copies):
+        copy.wait()
+        total = total + arrived[d]
+    totals[place] = total
+    for copy in back_copies:
         copy.start()
     mask = score_mask(rc_ref[:, :1], rr_ref[:1, :])
     fresh = rc_ref[:, :1] == 0
@@ -224,14 +400,6 @@
         step = step + headsum(x * v, g, per_group)
         through = decay_ref[:1, cols] * jnp.sum(sin * gin, axis=0, keepdims=True)
         kk = kk + headsum(jnp.broadcast_to(through, (8, width)), g, per_group)
-        if g == 0:
-            total = mine[place]
-            for d, copy in enumerate(out_copies):
-                copy.wait()
-                total = total + arrived[d]
-            totals[place] = total
-            for copy in back_copies:
-                copy.start()
     before = jnp.where(iota((rows, rows), 0) > iota((rows, rows), 1), 1.0, 0.0)
     glog = lax.dot_general(before, net, (((1,), (0,)), ((), ())), precision=highest, preferred_element_type=f32) + kk[:1]
     gdt = einv_ref[...] * step - padded(rate_ref[...]) * glog
@@ -241,159 +409,6 @@
         copy.wait()
     gdown_ref[...] = jnp.concatenate([totals[j] for j in range(ctx // 2)], axis=0).T
     gup_ref[...] = jnp.concatenate([totals[j] for j in range(ctx // 2, ctx)], axis=0)
-
-
-CHUNK = 16
-
-
-def remote(src, dst, send, recv, target):
-    return pltpu.make_async_remote_copy(
-        src_ref=src, dst_ref=dst, send_sem=send, recv_sem=recv, device_id=target,
-        device_id_type=pl.DeviceIdType.MESH,
-    )
-
-
-def group_peers():
-    inner = lax.axis_size("fsdp")
-    count = lax.axis_size("head") * inner
-    me = lax.axis_index("head") * inner + lax.axis_index("fsdp")
-    ids = [lax.rem(me + d, count) for d in range(1, count)]
-    return [{"head": lax.div(i, inner), "fsdp": lax.rem(i, inner)} for i in ids]
-
-
-def greet():
-    ctx = lax.axis_size("ctx")
-    place = lax.axis_index("ctx")
-    barrier = pltpu.get_barrier_semaphore()
-    peers = group_peers()
-    for peer in peers:
-        pl.semaphore_signal(barrier, inc=1, device_id=peer, device_id_type=pl.DeviceIdType.MESH)
-
-    @pl.when(place > 0)
-    def _():
-        pl.semaphore_signal(barrier, inc=1, device_id={"ctx": place - 1}, device_id_type=pl.DeviceIdType.MESH)
-
-    @pl.when(place < ctx - 1)
-    def _():
-        pl.semaphore_signal(barrier, inc=1, device_id={"ctx": place + 1}, device_id_type=pl.DeviceIdType.MESH)
-
-    ends = (place == 0) | (place == ctx - 1)
-
-    @pl.when(ends)
-    def _():
-        pl.semaphore_wait(barrier, len(peers) + 1)
-
-    @pl.when(jnp.logical_not(ends))
-    def _():
-        pl.semaphore_wait(barrier, len(peers) + 2)
-
-
-def exchange(part_ref, box, send, recv):
-    return [remote(part_ref, box.at[d], send.at[d], recv.at[d], peer) for d, peer in enumerate(group_peers())]
-
-
-def gathered_sum(part_ref, box):
-    total = part_ref[...]
-    for d in range(box.shape[0]):
-        total = total + box[d]
-    return (adapter_scale * total).astype(bf16)
-
-
-def chain_step(k, first, last, target, inbox, outbox, send, recv, decay, own_ref):
-    copy = remote(outbox.at[k], inbox.at[k], send.at[k], recv.at[k], target)
-
-    @pl.when(first)
-    def _():
-        inbox[k] = jnp.zeros(inbox.shape[1:], f32)
-
-    @pl.when(jnp.logical_not(first))
-    def _():
-        copy.wait_recv()
-
-    @pl.when(jnp.logical_not(last))
-    def _():
-        outbox[k] = decay * inbox[k] + own_ref[CHUNK * k : CHUNK * (k + 1), :]
-        copy.start()
-
-    return copy
-
-
-def start_kernel(part_ref, state_ref, decay_ref, gu_ref, sin_ref, box, inbox, outbox, gsend, grecv, send, recv):
-    ctx = lax.axis_size("ctx")
-    place = lax.axis_index("ctx")
-    first, last = place == 0, place == ctx - 1
-    greet()
-    swaps = exchange(part_ref, box, gsend, grecv)
-    decay = decay_ref[:1, :]
-    target = {"ctx": lax.rem(place + 1, ctx)}
-    copies = []
-    for k in range(inbox.shape[0]):
-        copies.append(chain_step(k, first, last, target, inbox, outbox, send, recv, decay, state_ref))
-        if k == 0:
-            for swap in swaps:
-                swap.start()
-        sin_ref[CHUNK * k : CHUNK * (k + 1), :] = inbox[k]
-    for swap in swaps:
-        swap.wait()
-    gu_ref[...] = gathered_sum(part_ref, box)
-
-    @pl.when(jnp.logical_not(last))
-    def _():
-        for copy in copies:
-            copy.wait_send()
-
-
-def middle_kernel(part_ref, up_ref, gout_ref, ginj_ref, decay_ref, gin_ref, out_ref, dup_ref,
-                  box, inbox, outbox, usend, urecv, send, recv):
-    ctx = lax.axis_size("ctx")
-    place = lax.axis_index("ctx")
-    first, last = place == 0, place == ctx - 1
-    chunks = inbox.shape[0]
-    below = {"ctx": lax.rem(place + ctx - 1, ctx)}
-    greet()
-    swaps = exchange(part_ref, box, usend, urecv)
-    copies = [remote(outbox.at[k], inbox.at[k], send.at[k], recv.at[k], below) for k in range(chunks)]
-
-    def adapter():
-        for swap in swaps:
-            swap.wait()
-        u = gathered_sum(part_ref, box)
-        out_ref[...] = tn(u, up_ref[...]).astype(bf16)
-        dup_ref[...] = nn(u, gout_ref[...])
-
-    @pl.when(last)
-    def _():
-        for k in range(chunks):
-            outbox[k] = ginj_ref[CHUNK * k : CHUNK * (k + 1), :]
-            copies[k].start()
-        gin_ref[...] = jnp.zeros_like(gin_ref)
-
-    for swap in swaps:
-        swap.start()
-
-    @pl.when(first)
-    def _():
-        adapter()
-
-    decay = decay_ref[:1, :]
-
-    @pl.when(jnp.logical_not(last))
-    def _():
-        for k in range(chunks):
-            copies[k].wait_recv()
-
-            @pl.when(jnp.logical_not(first))
-            def _():
-                outbox[k] = decay * inbox[k] + ginj_ref[CHUNK * k : CHUNK * (k + 1), :]
-                copies[k].start()
-
-            gin_ref[CHUNK * k : CHUNK * (k + 1), :] = inbox[k]
-
-    @pl.when(jnp.logical_not(first))
-    def _():
-        adapter()
-        for k in range(chunks):
-            copies[k].wait_send()
 
 
 def call(kernel, name, outs, args, scratch=(), collective_id=None):
@@ -441,21 +456,16 @@
          ((rank, channels), f32), ((rank, rows), f32)],
         (x, z, b, c, gx, e, einv, dt, rc, rr, em, skip_row, gain_row, down_rows, gu, sin),
     )
-    gin, adapter_output, dup = call(
-        middle_kernel, "middle",
-        [((STATE, channels), f32), ((rows, channels), bf16), ((rank, channels), f32)],
-        (u_part, up, gout, ginj, decay),
-        [swap, slab, slab] + [dma((peers,))] * 2 + [dma((chunks,))] * 2, 2,
-    )
     ctx = lax.axis_size("ctx")
     share = STATE // ctx
-    dx, db, dc, dstep, gdown, gup = call(
+    dx, db, dc, dstep, gdown, gup, adapter_output = call(
         lambda *r: backward_kernel(heads, *r), "backward",
         [((rows, channels), bf16), (b.shape, bf16), (c.shape, bf16), ((heads, rows), f32),
-         ((channels, rank), f32), ((rank, channels), f32)],
-        (x, b, c, e, einv, dt, rc, rr, em, skip_row, rate_row, gy, gd, sin, pn, kk, gin, decay, ddown, dup),
-        [pltpu.VMEM((ctx, share, channels), f32), pltpu.VMEM((ctx - 1, share, channels), f32),
-         pltpu.VMEM((ctx, share, channels), f32)] + [dma((ctx - 1,))] * 4, 3,
+         ((channels, rank), f32), ((rank, channels), f32), ((rows, channels), bf16)],
+        (x, b, c, e, einv, dt, rc, rr, em, skip_row, rate_row, gy, gd, sin, pn, kk, decay, ddown, u_part, up, gout, ginj),
+        [pltpu.VMEM((STATE, channels), f32), swap, slab, slab] + [dma((peers,))] * 2 + [dma((chunks,))] * 2
+        + [pltpu.VMEM((ctx, share, channels), f32), pltpu.VMEM((ctx - 1, share, channels), f32),
+           pltpu.VMEM((ctx, share, channels), f32)] + [dma((ctx - 1,))] * 4, 3,
     )
     return mixed, adapter_output, dx, dz, db, dc, dstep, gdown, gup
 

time: 104 us -> 101 us (0.971)
  the two profiles are of different devices: /device:TPU:0 before, /device:TPU:28 now
where the time goes in v3:
time: 101 us
  Pallas kernels  90 us (89%)
  local copies, waits for them, and re-layouts  8.05 us (8%)
  matrix products  2.41 us (2%)
    pallas_call x4, Pallas kernels, call(): pl.pallas_call(kernel, name=name, out_shape=[jax.ShapeDtypeStruct(s, d) f...  90 us
    unnamed x17, local copies, waits for them, and re-layouts  8.05 us
    dot_general x1, matrix products, nt(): lax.dot_general(a, b, (((1,), (1,)), ((), ())), preferred_element_type=f32)  2.41 us

profile of v3, /device:TPU:28, one launch (start us, length us, event | category | flops | bytes accessed | tf_op | source)
XLA Modules:
  0.0 101.1 jit_solution(12684669675348529861)
XLA Ops:
  0.6 2.4 %fusion.part_ref = f32[64,512]{1,0:T(8,128)} fusion(bf16[64,1024]{1,0:T(8,128)(2,1)} %r_19_.1, bf16[512,1024]{1,0:T(8,128)(2,1)} %r_20_.1), kind=kOutput, calls=%fused_computation | convolution fusion | flops 67108864 | bytes 1310720 | tf_op jit(solution)/shard_map/dot_general | solution.py:22
  3.0 5.7 %scan.1 = (f32[512,128]{1,0:T(8,128)}, f32[512,128]{1,0:T(8,128)}, f32[512,128]{1,0:T(8,128)}, f32[512,128]{1,0:T(8,128)}, f32[8,512]{1,0:T(8,128)}, /*index=5*/...) custom-call(bf16[512,1024]{1,0:T(8,128)(2,1)} %r_0_.3, bf16[512,256]{1,0:T(8,128)(2,1)} %r_1_.3, ...), custom_call_target="tpu_custom_call" | custom-call | tf_op jit(solution)/shard_map/scan/pallas_call | solution.py:417
  8.7 21.2 %start.1 = (bf16[64,512]{1,0:T(8,128)(2,1)}, f32[128,1024]{1,0:T(8,128)}) custom-call(f32[64,512]{1,0:T(8,128)} %fusion.part_ref, f32[128,1024]{1,0:T(8,128)} %get-tuple-element.41.state_ref, f32[8,1024]{1,0:T(8,128)} %get-tuple-element.42.decay_ref.r_16_), custom_call_target="tpu_custom_call" | custom-call | tf_op jit(solution)/shard_map/start/pallas_call | solution.py:417
  29.9 11.2 %forward.1 = (bf16[512,1024]{1,0:T(8,128)(2,1)}, bf16[512,1024]{1,0:T(8,128)(2,1)}, f32[512,1024]{1,0:T(8,128)}, bf16[512,1024]{1,0:T(8,128)(2,1)}, f32[128,1024...) custom-call(bf16[512,1024]{1,0:T(8,128)(2,1)} %r_0_.3, ...), custom_call_target="tpu_custom_call" | custom-call | tf_op jit(solution)/shard_map/forward/pallas_call | solution.py:417
  41.1 52.0 %backward.1 = (bf16[512,1024]{1,0:T(8,128)(2,1)}, bf16[512,256]{1,0:T(8,128)(2,1)}, bf16[512,256]{1,0:T(8,128)(2,1)}, f32[16,512]{1,0:T(8,128)}, f32[1024,64]{1,...) custom-call(bf16[512,1024]{1,0:T(8,128)(2,1)} %r_0_.3, bf16[512,256]{1,0:T(8,128)(2,1)} %r_1_.3, ...), custom_call_target="tpu_custom_call" | custom-call | tf_op jit(solution)/shard_map/backward/pallas_call | solution.py:417
  93.1 0.0 copy-start
  93.1 2.0 %copy.23 = f32[1024,64]{0,1:T(8,128)} copy(f32[1024,64]{1,0:T(8,128)} %get-tuple-element.68) | data formatting | bytes 524288
  95.1 0.0 copy-start.3
  95.1 0.0 copy-start.2
  95.1 2.3 %copy.30 = bf16[512,1024]{1,0:T(8,128)(2,1)} copy(bf16[512,1024]{1,0:T(8,128)(2,1)} %get-tuple-element.80) | data formatting | bytes 2097152
  97.4 0.0 copy-done
  97.4 0.0 copy-start.4
  97.4 0.0 copy-start.1
  97.4 1.0 copy.31
  98.4 0.0 copy-done.3
  98.4 0.7 copy.32
  99.1 0.0 copy-done.2
  99.1 0.7 copy.33
  99.8 0.0 copy-done.4
  99.8 0.6 copy.34
  100.4 0.0 copy-done.1
  100.4 0.7 copy.35
Async XLA Ops:
  93.1 4.4 %copy-start = (bf16[512,1024]{1,0:T(8,128)(2,1)S(1)}, bf16[512,1024]{1,0:T(8,128)(2,1)}, u32[]{:S(2)}) copy-start(bf16[512,1024]{1,0:T(8,128)(2,1)} %get-tuple-element.81) | copy-start | bytes 3145732
  95.1 3.3 %copy-start.3 = (bf16[512,256]{1,0:T(8,128)(2,1)S(1)}, bf16[512,256]{1,0:T(8,128)(2,1)}, u32[]{:S(2)}) copy-start(bf16[512,256]{1,0:T(8,128)(2,1)} %get-tuple-element.83) | copy-start | bytes 786436
  95.1 4.0 %copy-start.2 = (bf16[512,256]{1,0:T(8,128)(2,1)S(1)}, bf16[512,256]{1,0:T(8,128)(2,1)}, u32[]{:S(2)}) copy-start(bf16[512,256]{1,0:T(8,128)(2,1)} %get-tuple-element.84) | copy-start | bytes 786436
  97.4 2.4 %copy-start.4 = (f32[16,512]{1,0:T(8,128)S(1)}, f32[16,512]{1,0:T(8,128)}, u32[]{:S(2)}) copy-start(f32[16,512]{1,0:T(8,128)} %get-tuple-element.85) | copy-start | bytes 98308
  97.4 3.0 %copy-start.1 = (f32[64,1024]{1,0:T(8,128)S(1)}, f32[64,1024]{1,0:T(8,128)}, u32[]{:S(2)}) copy-start(f32[64,1024]{1,0:T(8,128)} %get-tuple-element.87) | copy-start | bytes 786436
